TPU v7x, 256 devices: a whole 4x4x8 slice. The times are simulated.
256 devices in a mesh: shot: 4 (over y_lo, core), dom: 64 (over x, y_hi, z).
Axes of the slice: x: 4, y: 4 (y_hi: 2, y_lo: 2; y = y_hi * 2 + y_lo), z: 8, core: 2. Of those that a mesh axis runs over, the one named last changes fastest.
Arguments:
- wave_before: float32 [4, 1024, 64, 256], P('shot', 'dom'), may hold values from -1.5 to 1.5
- wave_current: float32 [4, 1024, 64, 256], P('shot', 'dom'), may hold values from -1.5 to 1.5
- adjoint_far: float32 [4, 1024, 64, 256], P('shot', 'dom'), may hold values from -1.5 to 1.5
- adjoint_near: float32 [4, 1024, 64, 256], P('shot', 'dom'), may hold values from -1.5 to 1.5
- labels: int32 [1024, 64, 256], P('dom'), may hold values from 0 to 7
- table: float32 [8], replicated, may hold values from 0.03 to 0.12
- source_index: int32 [4, 3], P('shot'), may hold values from 0 to 1023, as said below
- wavelet: float32 [4, 4], P('shot'), may hold values from -6 to 6
- receiver_index: int32 [4, 1024, 3], P('shot'), may hold values from 0 to 1023, as said below
- residual: float32 [4, 4, 1024], P('shot'), may hold values from -6 to 6
Outputs:
- final_wave: float32 [4, 1024, 64, 256], P('shot', 'dom')
- first_adjoint: float32 [4, 1024, 64, 256], P('shot', 'dom')
- gradient: float32 [1024, 64, 256], P('dom')
Inputs may be any that keep to these rules, and one draw needn't show every extreme that they name: `source_index`: column 0 is a cell index along x below 1024, column 1 along z below 64, column 2 along y below 256. The first shot's source lies at the far corner of the grid and the second shot's source at depth 0. `receiver_index`: last index 0 is a cell index along x below 1024, 1 along z below 64, 2 along y below 256; receivers may share a cell. In every shot the first receiver lies at the far corner of the grid and the second at depth 0.
All inputs are finite; a program needn't handle non-finite values.
Results may differ from a plain program's by a relative error of at most 0.00002.
Values sent between devices are 32-bit elements; how exact they have to be, the bound alone decides.
A program may use at most 128 MiB of HBM per device.

v0:
```python
import jax
import jax.numpy as jnp
from jax import lax
from jax.sharding import PartitionSpec as P

centre_coef = -205.0 / 72.0
side_coefs = (8.0 / 5.0, -1.0 / 5.0, 8.0 / 315.0, -1.0 / 560.0)


def padded(block, sides, width):
    for axis, dim in sides:
        count = lax.axis_size(axis)
        forward = [(i, i + 1) for i in range(count - 1)]
        backward = [(target, source) for source, target in forward]
        low = lax.ppermute(
            lax.slice_in_dim(block, block.shape[dim] - width, None, axis=dim), axis, forward
        )
        high = lax.ppermute(lax.slice_in_dim(block, 0, width, axis=dim), axis, backward)
        block = jnp.concatenate([low, block, high], axis=dim)
    return block


def stencil(extended, centre):
    planes = centre.shape[1]
    depth = centre.shape[2]
    across = centre.shape[3]
    padded_yz = jnp.pad(centre, ((0, 0), (0, 0), (4, 4), (4, 4)))
    result = 3.0 * centre_coef * centre
    for k in range(1, 5):
        coef = side_coefs[k - 1]
        result = result + coef * (
            extended[:, 4 + k : 4 + k + planes]
            + extended[:, 4 - k : 4 - k + planes]
            + padded_yz[:, :, 4 + k : 4 + k + depth, 4 : 4 + across]
            + padded_yz[:, :, 4 - k : 4 - k + depth, 4 : 4 + across]
            + padded_yz[:, :, 4 : 4 + depth, 4 + k : 4 + k + across]
            + padded_yz[:, :, 4 : 4 + depth, 4 - k : 4 - k + across]
        )
    return result


def rates(labels, table):
    result = jnp.zeros(labels.shape, jnp.float32)
    for region in range(table.shape[0]):
        result = result + jnp.where(labels == region, table[region], jnp.zeros((), jnp.float32))
    return result


def inject(field_in, index_x, index_z, index_y, values, first_plane, planes):
    local_x = index_x - first_plane
    valid = (local_x >= 0) & (local_x < planes)
    local_x = jnp.where(valid, local_x, planes)
    return field_in.at[0, local_x, index_z, index_y].add(values, mode="drop")


def per_device(
    wave_before,
    wave_current,
    adjoint_far,
    adjoint_near,
    labels,
    table,
    source_index,
    wavelet,
    receiver_index,
    residual,
):
    planes = wave_current.shape[1]
    first_plane = lax.axis_index("dom") * planes
    steps_count = wavelet.shape[1]
    rate = rates(labels, table)[None]
    source_x = source_index[0, 0]
    source_z = source_index[0, 1]
    source_y = source_index[0, 2]
    receiver_x = receiver_index[0, :, 0]
    receiver_z = receiver_index[0, :, 1]
    receiver_y = receiver_index[0, :, 2]
    gradient = jnp.zeros_like(wave_current)
    stored = []
    previous, current = (wave_before, wave_current)
    for step in range(steps_count):
        extended = padded(current, (("dom", 1),), 4)
        lap_current = stencil(extended, current)
        stored.append(lap_current)
        upcoming = 2.0 * current - previous + rate * lap_current
        upcoming = inject(
            upcoming, source_x, source_z, source_y, wavelet[0, step], first_plane, planes
        )
        previous, current = (current, upcoming)
    later, adjoint = (adjoint_far, adjoint_near)
    for step in reversed(range(steps_count)):
        gradient = gradient + adjoint * stored[step]
        scaled = rate * adjoint
        extended = padded(scaled, (("dom", 1),), 4)
        earlier = 2.0 * adjoint - later + stencil(extended, scaled)
        earlier = inject(
            earlier, receiver_x, receiver_z, receiver_y, residual[0, step], first_plane, planes
        )
        later, adjoint = (adjoint, earlier)
    total = lax.psum(gradient[0], "shot")
    return (current, adjoint, total)


def solution(mesh):
    placed = (
        P("shot", "dom", None, None),
        P("shot", "dom", None, None),
        P("shot", "dom", None, None),
        P("shot", "dom", None, None),
        P("dom", None, None),
        P(),
        P("shot", None),
        P("shot", None),
        P("shot", None, None),
        P("shot", None, None),
    )
    return jax.shard_map(
        per_device,
        mesh=mesh,
        in_specs=placed,
        out_specs=(
            P("shot", "dom", None, None),
            P("shot", "dom", None, None),
            P("dom", None, None),
        ),
        check_vma=False,
    )
```

profile of v0, /device:TPU:7, one launch (start us, length us, event | category | flops | bytes accessed | tf_op | source)
XLA Modules:
  0.0 309.9 jit_solution(7169597570799639092)
XLA Ops:
  7.2 1.9 fusion.278
  9.2 10.4 %collective-permute-start = (f32[1,4,64,256]{3,2,1,0:T(8,128)}, f32[1,4,64,256]{3,2,1,0:T(8,128)}, u32[]{:S(2)}, u32[]{:S(2)}) collective-permute-start(f32[1,4,64,256]{3,2,1,0:T(8,128)} %get-tuple-element.69), channel_id=1, source_target_pairs={{1,0},{2,1},{3,2},{4,3},{5,4},{6,5},{7,6},{8,7},{9,8},{10,9},{11,1... | collective-permute-start | bytes 786440 | tf_op jit(solution)/shard_map/ppermute | solution.py:18
  19.5 1.9 collective-permute-start.1
  21.5 1.6 fusion.285
  23.2 7.0 %bitcast_multiply_fusion.3 = f32[1,16,64,256]{3,2,1,0:T(8,128)S(1)} fusion(f32[1,16,64,256]{3,2,1,0:T(8,128)} %param.21, f32[]{:T(128)} %bitcast.7, s32[16,64,256]{2,1,0:T(8,128)S(1)} %copy-done, f32[]{:T(128)} %bitcast.6, f32[]{:T(128)} %bitcast.5, f32[]{:T(128)} %bitcast.4, f32[]{:T(128)} %bitcast.3, f32[]{:T(128)} %bitcast.2, f32[]{:T(128)} %bitcast.1, ...), kind=kLoop, calls=%fused_computation.503 | loop fusion | flops 6291456 | bytes 3145760 | tf_op jit(solution)/shard_map/mul | solution.py:93
  30.2 0.8 fusion.281
  31.0 7.9 %collective-permute-start.8 = (f32[1,4,64,256]{3,2,1,0:T(8,128)}, f32[1,4,64,256]{3,2,1,0:T(8,128)S(1)}, u32[]{:S(2)}, u32[]{:S(2)}) collective-permute-start(f32[1,4,64,256]{3,2,1,0:T(8,128)} %get-tuple-element.77), channel_id=1, source_target_pairs={{1,0},{2,1},{3,2},{4,3},{5,4},{6,5},{7,6},{8,7},{9,8},{10,9},{11,1... | collective-permute-start | bytes 786440 | tf_op jit(solution)/shard_map/ppermute | solution.py:18
  38.9 1.9 collective-permute-start.9
  40.8 0.6 fusion.284
  46.0 0.8 and_reduce_fusion.1
  46.7 0.7 fusion.283
  47.4 4.4 %collective-permute-done.9 = f32[1,4,64,256]{3,2,1,0:T(8,128)} collective-permute-done((f32[1,4,64,256]{3,2,1,0:T(8,128)}, f32[1,4,64,256]{3,2,1,0:T(8,128)}, u32[]{:S(2)}, u32[]{:S(2)}) %collective-permute-start.9) | collective-permute-done | bytes 262176 | tf_op jit(solution)/shard_map/ppermute | solution.py:15
  51.9 5.0 %fusion.96 = f32[1,16,64,256]{3,2,1,0:T(8,128)S(1)} fusion(f32[1,16,64,256]{3,2,1,0:T(8,128)S(1)} %bitcast_multiply_fusion.3, f32[1,4,64,256]{3,2,1,0:T(8,128)} %collective-permute-done.9, f32[1,4,64,256]{3,2,1,0:T(8,128)S(1)} %collective-permute-done.8, f32[1,16,64,256]{3,2,1,0:T(8,128)} %param.20, f32[1,16,64,256]{3,2,1,0:T(8,128)S(1)} %copy-done.4), kind=kLoop, calls=%fused_computation.312 | loop fusion | flops 10485760 | bytes 4718592 | tf_op jit(solution)/shard_map/add | solution.py:95
  57.4 6.5 %scatter_fusion = f32[262144]{0:T(1024)S(1)} fusion(f32[262144]{0:T(1024)S(1)} %bitcast.57, s32[1024]{0:T(1024)S(1)} %broadcast_select_fusion, f32[1024]{0:T(1024)S(1)} %bitcast.67), kind=kCustom, calls=%fused_computation | custom fusion | flops 1024 | bytes 16384
  64.2 5.7 %bitcast_multiply_fusion.2 = f32[1,16,64,256]{3,2,1,0:T(8,128)S(1)} fusion(f32[1,16,64,256]{3,2,1,0:T(8,128)S(1)} %reshape.240, f32[]{:T(128)} %bitcast.7, s32[16,64,256]{2,1,0:T(8,128)S(1)} %copy-done, f32[]{:T(128)} %bitcast.6, f32[]{:T(128)} %bitcast.5, f32[]{:T(128)} %bitcast.4, f32[]{:T(128)} %bitcast.3, f32[]{:T(128)} %bitcast.2, f32[]{:T(128)} %bitcast.1, ...), kind=kLoop, calls=%fused_computation.502 | loop fusion | flops 6291456 | bytes 3145760 | tf_op jit(solution)/shard_map/mul | solution.py:93
  69.9 0.8 fusion.280
  70.7 3.6 %collective-permute-start.10 = (f32[1,4,64,256]{3,2,1,0:T(8,128)}, f32[1,4,64,256]{3,2,1,0:T(8,128)S(1)}, u32[]{:S(2)}, u32[]{:S(2)}) collective-permute-start(f32[1,4,64,256]{3,2,1,0:T(8,128)} %get-tuple-element.75), channel_id=1, source_target_pairs={{1,0},{2,1},{3,2},{4,3},{5,4},{6,5},{7,6},{8,7},{9,8},{10,9},{11,1... | collective-permute-start | bytes 786440 | tf_op jit(solution)/shard_map/ppermute | solution.py:18
  74.3 1.9 collective-permute-start.11
  76.3 1.0 constant_dynamic-update-slice_fusion.3
  77.6 1.0 constant_dynamic-update-slice_fusion
  78.6 8.7 %fusion.266 = (f32[1,16,64,256]{3,2,1,0:T(8,128)S(1)}, f32[1,16,64,256]{3,2,1,0:T(8,128)}) fusion(f32[1,16,64,256]{3,2,1,0:T(8,128)S(1)} %copy-done.15, f32[1,16,64,256]{3,2,1,0:T(8,128)S(1)} %copy-done.11, f32[]{:T(128)} %bitcast.7, s32[16,64,256]{2,1,0:T(8,128)S(1)} %copy-done, f32[]{:T(128)} %bitcast.6, f32[]{:T(128)} %bitcast.5, f32[]{:T(128)} %bitcast.4, ...), kind=kLoop, calls=%fused_computation.508 | loop fusion | flops 14680064 | bytes 13631520 | tf_op jit(solution)/shard_map/add | solution.py:85
  87.3 1.0 copy-done.6
  88.2 1.3 fusion.286
  91.5 1.4 scatter-add.48
  92.8 1.9 fusion.277
  94.7 7.9 %collective-permute-start.2 = (f32[1,4,64,256]{3,2,1,0:T(8,128)}, f32[1,4,64,256]{3,2,1,0:T(8,128)}, u32[]{:S(2)}, u32[]{:S(2)}) collective-permute-start(f32[1,4,64,256]{3,2,1,0:T(8,128)} %get-tuple-element.67), channel_id=1, source_target_pairs={{1,0},{2,1},{3,2},{4,3},{5,4},{6,5},{7,6},{8,7},{9,8},{10,9},{11,1... | collective-permute-start | bytes 786440 | tf_op jit(solution)/shard_map/ppermute | solution.py:18
  102.5 2.1 collective-permute-start.3
  104.7 15.0 %fusion.67 = f32[1,16,64,256]{3,2,1,0:T(8,128)S(1)} fusion(f32[1,16,64,256]{3,2,1,0:T(8,128)} %copy-done.12, f32[1,4,64,256]{3,2,1,0:T(8,128)} %collective-permute-done.11, f32[1,4,64,256]{3,2,1,0:T(8,128)S(1)} %collective-permute-done.10, f32[1,16,64,256]{3,2,1,0:T(8,128)S(1)} %copy-done.5, f32[1,16,64,256]{3,2,1,0:T(8,128)S(1)} %reshape.240), kind=kLoop, calls=%fused_computation.283 | loop fusion | flops 10485760 | bytes 4718592 | tf_op jit(solution)/shard_map/add | solution.py:95
  120.2 6.5 %scatter_fusion.1 = f32[262144]{0:T(1024)S(1)} fusion(f32[262144]{0:T(1024)S(1)} %bitcast.58, s32[1024]{0:T(1024)S(1)} %broadcast_select_fusion, f32[1024]{0:T(1024)S(1)} %bitcast.66), kind=kCustom, calls=%fused_computation.1 | custom fusion | flops 1024 | bytes 16384
  126.7 1.3 reshape.244
  127.9 21.6 %fusion.267 = (f32[1,16,64,256]{3,2,1,0:T(8,128)S(1)}, f32[1,16,64,256]{3,2,1,0:T(8,128)}) fusion(f32[1,16,64,256]{3,2,1,0:T(8,128)} %param.19, f32[1,16,64,256]{3,2,1,0:T(8,128)} %scatter-add.48, f32[]{:T(128)} %bitcast.7, s32[16,64,256]{2,1,0:T(8,128)S(1)} %copy-done, f32[]{:T(128)} %bitcast.6, f32[]{:T(128)} %bitcast.5, f32[]{:T(128)} %bitcast.4, ...), kind=kLoop, calls=%fused_computation.509 | loop fusion | flops 16777216 | bytes 5767200 | tf_op jit(solution)/shard_map/add | solution.py:85
  149.6 1.0 copy-done.8
  150.5 1.2 fusion.287
  153.7 1.4 scatter-add.49
  155.1 1.1 fusion.276
  156.1 7.9 %collective-permute-start.4 = (f32[1,4,64,256]{3,2,1,0:T(8,128)S(1)}, f32[1,4,64,256]{3,2,1,0:T(8,128)S(1)}, u32[]{:S(2)}, u32[]{:S(2)}) collective-permute-start(f32[1,4,64,256]{3,2,1,0:T(8,128)S(1)} %get-tuple-element.65), channel_id=1, source_target_pairs={{1,0},{2,1},{3,2},{4,3},{5,4},{6,5},{7,6},{8,7},{9,8},{10,9},{11,1... | collective-permute-start | bytes 786440 | tf_op jit(solution)/shard_map/ppermute | solution.py:18
  164.0 1.9 collective-permute-start.5
  166.0 5.8 %bitcast_multiply_fusion.1 = f32[1,16,64,256]{3,2,1,0:T(8,128)S(1)} fusion(f32[1,16,64,256]{3,2,1,0:T(8,128)S(1)} %copy-done.1, f32[]{:T(128)} %bitcast.7, s32[16,64,256]{2,1,0:T(8,128)S(1)} %copy-done, f32[]{:T(128)} %bitcast.6, f32[]{:T(128)} %bitcast.5, f32[]{:T(128)} %bitcast.4, f32[]{:T(128)} %bitcast.3, f32[]{:T(128)} %bitcast.2, f32[]{:T(128)} %bitcast.1, ...), kind=kLoop, calls=%fused_computation.501 | loop fusion | flops 6291456 | bytes 3145760 | tf_op jit(solution)/shard_map/mul | solution.py:93
  171.8 0.8 fusion.279
  172.6 8.0 %collective-permute-start.12 = (f32[1,4,64,256]{3,2,1,0:T(8,128)}, f32[1,4,64,256]{3,2,1,0:T(8,128)S(1)}, u32[]{:S(2)}, u32[]{:S(2)}) collective-permute-start(f32[1,4,64,256]{3,2,1,0:T(8,128)} %get-tuple-element.73), channel_id=1, source_target_pairs={{1,0},{2,1},{3,2},{4,3},{5,4},{6,5},{7,6},{8,7},{9,8},{10,9},{11,1... | collective-permute-start | bytes 786440 | tf_op jit(solution)/shard_map/ppermute | solution.py:18
  180.6 1.9 collective-permute-start.13
  182.6 10.3 %fusion.268 = (f32[1,16,64,256]{3,2,1,0:T(8,128)S(1)}, f32[1,16,64,256]{3,2,1,0:T(8,128)}) fusion(f32[1,16,64,256]{3,2,1,0:T(8,128)S(1)} %copy-done.7, f32[1,16,64,256]{3,2,1,0:T(8,128)S(1)} %copy-done.9, f32[]{:T(128)} %bitcast.7, s32[16,64,256]{2,1,0:T(8,128)S(1)} %copy-done, f32[]{:T(128)} %bitcast.6, f32[]{:T(128)} %bitcast.5, f32[]{:T(128)} %bitcast.4, ...), kind=kLoop, calls=%fused_computation.510 | loop fusion | flops 16777216 | bytes 5767200 | tf_op jit(solution)/shard_map/add | solution.py:85
  192.9 1.0 copy-done.10
  193.9 1.3 fusion.288
  197.2 1.4 scatter-add.50
  198.6 1.9 fusion.275
  200.5 7.9 %collective-permute-start.6 = (f32[1,4,64,256]{3,2,1,0:T(8,128)}, f32[1,4,64,256]{3,2,1,0:T(8,128)}, u32[]{:S(2)}, u32[]{:S(2)}) collective-permute-start(f32[1,4,64,256]{3,2,1,0:T(8,128)} %get-tuple-element.63), channel_id=1, source_target_pairs={{1,0},{2,1},{3,2},{4,3},{5,4},{6,5},{7,6},{8,7},{9,8},{10,9},{11,1... | collective-permute-start | bytes 786440 | tf_op jit(solution)/shard_map/ppermute | solution.py:18
  208.4 2.1 collective-permute-start.7
  210.6 4.9 %fusion.38 = f32[1,16,64,256]{3,2,1,0:T(8,128)S(1)} fusion(f32[1,16,64,256]{3,2,1,0:T(8,128)S(1)} %copy-done.14, f32[1,4,64,256]{3,2,1,0:T(8,128)} %collective-permute-done.13, f32[1,4,64,256]{3,2,1,0:T(8,128)S(1)} %collective-permute-done.12, f32[1,16,64,256]{3,2,1,0:T(8,128)S(1)} %reshape.240, f32[1,16,64,256]{3,2,1,0:T(8,128)S(1)} %copy-done.1), kind=kLoop, calls=%fused_computation.254 | loop fusion | flops 10485760 | bytes 4718592 | tf_op jit(solution)/shard_map/add | solution.py:95
  216.0 6.5 %scatter_fusion.2 = f32[262144]{0:T(1024)S(1)} fusion(f32[262144]{0:T(1024)S(1)} %bitcast.59, s32[1024]{0:T(1024)S(1)} %broadcast_select_fusion, f32[1024]{0:T(1024)S(1)} %bitcast.65), kind=kCustom, calls=%fused_computation.2 | custom fusion | flops 1024 | bytes 16384
  222.5 1.3 reshape.248
  223.7 18.2 %add_bitcast_fusion = (f32[16,64,256]{2,1,0:T(8,128)}, f32[1,16,64,256]{3,2,1,0:T(8,128)}) fusion(f32[1,16,64,256]{3,2,1,0:T(8,128)} %reshape.248, f32[1,16,64,256]{3,2,1,0:T(8,128)} %get-tuple-element.58, f32[1,16,64,256]{3,2,1,0:T(8,128)} %reshape.244, f32[1,16,64,256]{3,2,1,0:T(8,128)} %get-tuple-element.56, f32[1,16,64,256]{3,2,1,0:T(8,128)S(1)} %reshape.240, ...), kind=kLoop, calls=%fused_computation.512 | loop fusion | flops 11534336 | bytes 11010048 | tf_op jit(solution)/shard_map/squeeze | solution.py:100
  241.9 8.7 %bitcast_multiply_fusion = (f32[1,16,64,256]{3,2,1,0:T(8,128)S(1)}, f32[1,16,64,256]{3,2,1,0:T(8,128)}) fusion(f32[1,16,64,256]{3,2,1,0:T(8,128)S(1)} %copy-done.3, f32[]{:T(128)} %bitcast.7, s32[16,64,256]{2,1,0:T(8,128)S(1)} %copy-done, f32[]{:T(128)} %bitcast.6, f32[]{:T(128)} %bitcast.5, f32[]{:T(128)} %bitcast.4, f32[]{:T(128)} %bitcast.3, f32[]{:T(128)} %bitcast.2, ...), kind=kLoop, calls=%fused_computation.500 | loop fusion | flops 7340032 | bytes 7340064 | tf_op jit(solution)/shard_map/mul | solution.py:93
  250.6 0.8 fusion.274
  251.5 7.9 %collective-permute-start.14 = (f32[1,4,64,256]{3,2,1,0:T(8,128)}, f32[1,4,64,256]{3,2,1,0:T(8,128)S(1)}, u32[]{:S(2)}, u32[]{:S(2)}) collective-permute-start(f32[1,4,64,256]{3,2,1,0:T(8,128)} %get-tuple-element.59), channel_id=1, source_target_pairs={{1,0},{2,1},{3,2},{4,3},{5,4},{6,5},{7,6},{8,7},{9,8},{10,9},{11,1... | collective-permute-start | bytes 786440 | tf_op jit(solution)/shard_map/ppermute | solution.py:18
  259.3 1.9 collective-permute-start.15
  261.3 1.9 fusion.289
  265.1 1.4 scatter-add.51
  266.5 4.9 %collective-permute-done.15 = f32[1,4,64,256]{3,2,1,0:T(8,128)} collective-permute-done((f32[1,4,64,256]{3,2,1,0:T(8,128)}, f32[1,4,64,256]{3,2,1,0:T(8,128)}, u32[]{:S(2)}, u32[]{:S(2)}) %collective-permute-start.15) | collective-permute-done | bytes 262176 | tf_op jit(solution)/shard_map/ppermute | solution.py:15
  271.4 4.8 %fusion.9 = f32[1,16,64,256]{3,2,1,0:T(8,128)S(1)} fusion(f32[1,16,64,256]{3,2,1,0:T(8,128)S(1)} %get-tuple-element.61, f32[1,4,64,256]{3,2,1,0:T(8,128)} %collective-permute-done.15, f32[1,4,64,256]{3,2,1,0:T(8,128)S(1)} %collective-permute-done.14, f32[1,16,64,256]{3,2,1,0:T(8,128)S(1)} %copy-done.2, f32[1,16,64,256]{3,2,1,0:T(8,128)S(1)} %copy-done.3), kind=kLoop, calls=%fused_computation.225 | loop fusion | flops 10485760 | bytes 4718592 | tf_op jit(solution)/shard_map/add | solution.py:95
  276.8 6.5 %scatter_fusion.3 = f32[262144]{0:T(1024)S(1)} fusion(f32[262144]{0:T(1024)S(1)} %bitcast.56, s32[1024]{0:T(1024)S(1)} %broadcast_select_fusion, f32[1024]{0:T(1024)S(1)} %bitcast.64), kind=kCustom, calls=%fused_computation.3 | custom fusion | flops 1024 | bytes 16384
  283.2 1.3 reshape.252
  284.5 16.3 %all-reduce.10.cloned.1.call-done = f32[16,64,256]{2,1,0:T(8,128)} async-done(((f32[16,64,256]{2,1,0:T(8,128)}), f32[16,64,256]{2,1,0:T(8,128)}) %all-reduce.10.cloned.1.call-update) | async-done | bytes 1048592 | tf_op jit(solution)/shard_map/psum | solution.py:100
  300.8 2.3 copy.28
  (71 shorter events, 3.1 us)
Async XLA Ops:
  7.2 15.9 %copy-start = (s32[16,64,256]{2,1,0:T(8,128)S(1)}, s32[16,64,256]{2,1,0:T(8,128)}, u32[]{:S(2)}) copy-start(s32[16,64,256]{2,1,0:T(8,128)} %param.22) | copy-start | bytes 3145732
  7.2 293.6 %all-reduce.10.cloned.1.call-start = ((), (), s32[]{:S(2)}) async-start(), calls=%async_computation | async-start | bytes 2097152 | tf_op jit(solution)/shard_map/psum | solution.py:100
  9.2 68.4 %collective-permute-start = (f32[1,4,64,256]{3,2,1,0:T(8,128)}, f32[1,4,64,256]{3,2,1,0:T(8,128)}, u32[]{:S(2)}, u32[]{:S(2)}) collective-permute-start(f32[1,4,64,256]{3,2,1,0:T(8,128)} %get-tuple-element.69), channel_id=1, source_target_pairs={{1,0},{2,1},{3,2},{4,3},{5,4},{6,5},{7,6},{8,7},{9,8},{10,9},{11,1... | collective-permute-start | bytes 786440 | tf_op jit(solution)/shard_map/ppermute | solution.py:18
  19.5 56.7 %collective-permute-start.1 = (f32[1,4,64,256]{3,2,1,0:T(8,128)}, f32[1,4,64,256]{3,2,1,0:T(8,128)}, u32[]{:S(2)}, u32[]{:S(2)}) collective-permute-start(f32[1,4,64,256]{3,2,1,0:T(8,128)} %get-tuple-element.70), channel_id=1, source_target_pairs={{0,1},{1,2},{2,3},{3,4},{4,5},{5,6},{6,7},{7,8},{8,9},{9,10},{10,1... | collective-permute-start | bytes 786440 | tf_op jit(solution)/shard_map/ppermute | solution.py:15
  23.1 17.7 %copy-start.19 = (s32[1,3]{1,0:T(1,128)S(1)}, s32[1,3]{1,0:T(1,128)}, u32[]{:S(2)}) copy-start(s32[1,3]{1,0:T(1,128)} %param.24) | copy-start | bytes 40
  23.1 21.4 %copy-start.17 = (s32[1,1024,3]{1,0,2:T(1,128)S(1)}, s32[1,1024,3]{1,0,2:T(1,128)}, u32[]{:S(2)}) copy-start(s32[1,1024,3]{1,0,2:T(1,128)} %param.26) | copy-start | bytes 36868
  23.1 21.4 %copy-start.20 = (s32[4]{0:T(128)S(1)}, s32[4]{0:T(128)}, u32[]{:S(2)}) copy-start(s32[4]{0:T(128)} %constant.159) | copy-start | bytes 52
  23.1 21.5 %copy-start.22 = (s32[4]{0:T(128)S(1)}, s32[4]{0:T(128)}, u32[]{:S(2)}) copy-start(s32[4]{0:T(128)} %constant.156) | copy-start | bytes 52
  23.1 22.8 %copy-start.21 = (s32[4]{0:T(128)S(1)}, s32[4]{0:T(128)}, u32[]{:S(2)}) copy-start(s32[4]{0:T(128)} %constant.129.clone.1) | copy-start | bytes 52
  23.1 23.6 %copy-start.18 = (f32[1,4]{1,0:T(1,128)S(1)}, f32[1,4]{1,0:T(1,128)}, u32[]{:S(2)}) copy-start(f32[1,4]{1,0:T(1,128)} %param.25) | copy-start | bytes 52
  23.2 24.2 %copy-start.16 = (f32[1,4,1024]{2,1,0:T(4,128)S(1)}, f32[1,4,1024]{2,1,0:T(4,128)}, u32[]{:S(2)}) copy-start(f32[1,4,1024]{2,1,0:T(4,128)} %param.27) | copy-start | bytes 49156
  30.1 21.7 %copy-start.4 = (f32[1,16,64,256]{3,2,1,0:T(8,128)S(1)}, f32[1,16,64,256]{3,2,1,0:T(8,128)}, u32[]{:S(2)}) copy-start(f32[1,16,64,256]{3,2,1,0:T(8,128)} %param.21) | copy-start | bytes 3145732
  31.0 16.4 %collective-permute-start.8 = (f32[1,4,64,256]{3,2,1,0:T(8,128)}, f32[1,4,64,256]{3,2,1,0:T(8,128)S(1)}, u32[]{:S(2)}, u32[]{:S(2)}) collective-permute-start(f32[1,4,64,256]{3,2,1,0:T(8,128)} %get-tuple-element.77), channel_id=1, source_target_pairs={{1,0},{2,1},{3,2},{4,3},{5,4},{6,5},{7,6},{8,7},{9,8},{10,9},{11,1... | collective-permute-start | bytes 786440 | tf_op jit(solution)/shard_map/ppermute | solution.py:18
  38.9 13.0 %collective-permute-start.9 = (f32[1,4,64,256]{3,2,1,0:T(8,128)}, f32[1,4,64,256]{3,2,1,0:T(8,128)}, u32[]{:S(2)}, u32[]{:S(2)}) collective-permute-start(f32[1,4,64,256]{3,2,1,0:T(8,128)} %get-tuple-element.78), channel_id=1, source_target_pairs={{0,1},{1,2},{2,3},{3,4},{4,5},{5,6},{6,7},{7,8},{8,9},{9,10},{10,1... | collective-permute-start | bytes 786440 | tf_op jit(solution)/shard_map/ppermute | solution.py:15
  69.9 7.7 %copy-start.12 = (f32[1,16,64,256]{3,2,1,0:T(8,128)}, f32[1,16,64,256]{3,2,1,0:T(8,128)S(1)}, u32[]{:S(2)}) copy-start(f32[1,16,64,256]{3,2,1,0:T(8,128)S(1)} %bitcast_multiply_fusion.2) | copy-start | bytes 3145732
  69.9 7.4 %copy-start.11 = (f32[1,16,64,256]{3,2,1,0:T(8,128)S(1)}, f32[1,16,64,256]{3,2,1,0:T(8,128)}, u32[]{:S(2)}) copy-start(f32[1,16,64,256]{3,2,1,0:T(8,128)} %param.19) | copy-start | bytes 3145732
  70.7 33.9 %collective-permute-start.10 = (f32[1,4,64,256]{3,2,1,0:T(8,128)}, f32[1,4,64,256]{3,2,1,0:T(8,128)S(1)}, u32[]{:S(2)}, u32[]{:S(2)}) collective-permute-start(f32[1,4,64,256]{3,2,1,0:T(8,128)} %get-tuple-element.75), channel_id=1, source_target_pairs={{1,0},{2,1},{3,2},{4,3},{5,4},{6,5},{7,6},{8,7},{9,8},{10,9},{11,1... | collective-permute-start | bytes 786440 | tf_op jit(solution)/shard_map/ppermute | solution.py:18
  74.3 30.3 %collective-permute-start.11 = (f32[1,4,64,256]{3,2,1,0:T(8,128)}, f32[1,4,64,256]{3,2,1,0:T(8,128)}, u32[]{:S(2)}, u32[]{:S(2)}) collective-permute-start(f32[1,4,64,256]{3,2,1,0:T(8,128)} %get-tuple-element.76), channel_id=1, source_target_pairs={{0,1},{1,2},{2,3},{3,4},{4,5},{5,6},{6,7},{7,8},{8,9},{9,10},{10,1... | collective-permute-start | bytes 786440 | tf_op jit(solution)/shard_map/ppermute | solution.py:15
  77.3 1.3 copy-start.15
  87.2 1.0 copy-start.6
  87.2 17.4 %copy-start.5 = (f32[1,16,64,256]{3,2,1,0:T(8,128)S(1)}, f32[1,16,64,256]{3,2,1,0:T(8,128)}, u32[]{:S(2)}) copy-start(f32[1,16,64,256]{3,2,1,0:T(8,128)} %param.21) | copy-start | bytes 3145732
  94.7 33.3 %collective-permute-start.2 = (f32[1,4,64,256]{3,2,1,0:T(8,128)}, f32[1,4,64,256]{3,2,1,0:T(8,128)}, u32[]{:S(2)}, u32[]{:S(2)}) collective-permute-start(f32[1,4,64,256]{3,2,1,0:T(8,128)} %get-tuple-element.67), channel_id=1, source_target_pairs={{1,0},{2,1},{3,2},{4,3},{5,4},{6,5},{7,6},{8,7},{9,8},{10,9},{11,1... | collective-permute-start | bytes 786440 | tf_op jit(solution)/shard_map/ppermute | solution.py:18
  102.5 25.4 %collective-permute-start.3 = (f32[1,4,64,256]{3,2,1,0:T(8,128)}, f32[1,4,64,256]{3,2,1,0:T(8,128)}, u32[]{:S(2)}, u32[]{:S(2)}) collective-permute-start(f32[1,4,64,256]{3,2,1,0:T(8,128)} %get-tuple-element.68), channel_id=1, source_target_pairs={{0,1},{1,2},{2,3},{3,4},{4,5},{5,6},{6,7},{7,8},{8,9},{9,10},{10,1... | collective-permute-start | bytes 786440 | tf_op jit(solution)/shard_map/ppermute | solution.py:15
  149.5 1.0 copy-start.8
  149.6 16.4 %copy-start.1 = (f32[1,16,64,256]{3,2,1,0:T(8,128)S(1)}, f32[1,16,64,256]{3,2,1,0:T(8,128)}, u32[]{:S(2)}) copy-start(f32[1,16,64,256]{3,2,1,0:T(8,128)} %reshape.244) | copy-start | bytes 3145732
  156.1 26.4 %collective-permute-start.4 = (f32[1,4,64,256]{3,2,1,0:T(8,128)S(1)}, f32[1,4,64,256]{3,2,1,0:T(8,128)S(1)}, u32[]{:S(2)}, u32[]{:S(2)}) collective-permute-start(f32[1,4,64,256]{3,2,1,0:T(8,128)S(1)} %get-tuple-element.65), channel_id=1, source_target_pairs={{1,0},{2,1},{3,2},{4,3},{5,4},{6,5},{7,6},{8,7},{9,8},{10,9},{11,1... | collective-permute-start | bytes 786440 | tf_op jit(solution)/shard_map/ppermute | solution.py:18
  164.0 18.6 %collective-permute-start.5 = (f32[1,4,64,256]{3,2,1,0:T(8,128)S(1)}, f32[1,4,64,256]{3,2,1,0:T(8,128)S(1)}, u32[]{:S(2)}, u32[]{:S(2)}) collective-permute-start(f32[1,4,64,256]{3,2,1,0:T(8,128)S(1)} %get-tuple-element.66), channel_id=1, source_target_pairs={{0,1},{1,2},{2,3},{3,4},{4,5},{5,6},{6,7},{7,8},{8,9},{9,10},{10,1... | collective-permute-start | bytes 786440 | tf_op jit(solution)/shard_map/ppermute | solution.py:15
  165.9 16.6 %copy-start.9 = (f32[1,16,64,256]{3,2,1,0:T(8,128)S(1)}, f32[1,16,64,256]{3,2,1,0:T(8,128)}, u32[]{:S(2)}) copy-start(f32[1,16,64,256]{3,2,1,0:T(8,128)} %scatter-add.49) | copy-start | bytes 3145732
  171.8 10.8 %copy-start.13 = (f32[1,16,64,256]{3,2,1,0:T(8,128)}, f32[1,16,64,256]{3,2,1,0:T(8,128)S(1)}, u32[]{:S(2)}) copy-start(f32[1,16,64,256]{3,2,1,0:T(8,128)S(1)} %bitcast_multiply_fusion.1) | copy-start | bytes 3145732
  171.8 10.8 %copy-start.7 = (f32[1,16,64,256]{3,2,1,0:T(8,128)S(1)}, f32[1,16,64,256]{3,2,1,0:T(8,128)}, u32[]{:S(2)}) copy-start(f32[1,16,64,256]{3,2,1,0:T(8,128)} %scatter-add.48) | copy-start | bytes 3145732
  172.6 37.9 %collective-permute-start.12 = (f32[1,4,64,256]{3,2,1,0:T(8,128)}, f32[1,4,64,256]{3,2,1,0:T(8,128)S(1)}, u32[]{:S(2)}, u32[]{:S(2)}) collective-permute-start(f32[1,4,64,256]{3,2,1,0:T(8,128)} %get-tuple-element.73), channel_id=1, source_target_pairs={{1,0},{2,1},{3,2},{4,3},{5,4},{6,5},{7,6},{8,7},{9,8},{10,9},{11,1... | collective-permute-start | bytes 786440 | tf_op jit(solution)/shard_map/ppermute | solution.py:18
  180.6 29.9 %collective-permute-start.13 = (f32[1,4,64,256]{3,2,1,0:T(8,128)}, f32[1,4,64,256]{3,2,1,0:T(8,128)}, u32[]{:S(2)}, u32[]{:S(2)}) collective-permute-start(f32[1,4,64,256]{3,2,1,0:T(8,128)} %get-tuple-element.74), channel_id=1, source_target_pairs={{0,1},{1,2},{2,3},{3,4},{4,5},{5,6},{6,7},{7,8},{8,9},{9,10},{10,1... | collective-permute-start | bytes 786440 | tf_op jit(solution)/shard_map/ppermute | solution.py:15
  192.9 1.0 copy-start.10
  198.5 12.0 %copy-start.14 = (f32[1,16,64,256]{3,2,1,0:T(8,128)S(1)}, f32[1,16,64,256]{3,2,1,0:T(8,128)}, u32[]{:S(2)}) copy-start(f32[1,16,64,256]{3,2,1,0:T(8,128)} %copy-done.13) | copy-start | bytes 3145732
  200.5 23.2 %collective-permute-start.6 = (f32[1,4,64,256]{3,2,1,0:T(8,128)}, f32[1,4,64,256]{3,2,1,0:T(8,128)}, u32[]{:S(2)}, u32[]{:S(2)}) collective-permute-start(f32[1,4,64,256]{3,2,1,0:T(8,128)} %get-tuple-element.63), channel_id=1, source_target_pairs={{1,0},{2,1},{3,2},{4,3},{5,4},{6,5},{7,6},{8,7},{9,8},{10,9},{11,1... | collective-permute-start | bytes 786440 | tf_op jit(solution)/shard_map/ppermute | solution.py:18
  208.4 15.4 %collective-permute-start.7 = (f32[1,4,64,256]{3,2,1,0:T(8,128)}, f32[1,4,64,256]{3,2,1,0:T(8,128)}, u32[]{:S(2)}, u32[]{:S(2)}) collective-permute-start(f32[1,4,64,256]{3,2,1,0:T(8,128)} %get-tuple-element.64), channel_id=1, source_target_pairs={{0,1},{1,2},{2,3},{3,4},{4,5},{5,6},{6,7},{7,8},{8,9},{9,10},{10,1... | collective-permute-start | bytes 786440 | tf_op jit(solution)/shard_map/ppermute | solution.py:15
  223.7 18.2 %copy-start.3 = (f32[1,16,64,256]{3,2,1,0:T(8,128)S(1)}, f32[1,16,64,256]{3,2,1,0:T(8,128)}, u32[]{:S(2)}) copy-start(f32[1,16,64,256]{3,2,1,0:T(8,128)} %reshape.248) | copy-start | bytes 3145732
  250.6 20.8 %copy-start.2 = (f32[1,16,64,256]{3,2,1,0:T(8,128)S(1)}, f32[1,16,64,256]{3,2,1,0:T(8,128)}, u32[]{:S(2)}) copy-start(f32[1,16,64,256]{3,2,1,0:T(8,128)} %reshape.244) | copy-start | bytes 3145732
  251.5 15.0 %collective-permute-start.14 = (f32[1,4,64,256]{3,2,1,0:T(8,128)}, f32[1,4,64,256]{3,2,1,0:T(8,128)S(1)}, u32[]{:S(2)}, u32[]{:S(2)}) collective-permute-start(f32[1,4,64,256]{3,2,1,0:T(8,128)} %get-tuple-element.59), channel_id=1, source_target_pairs={{1,0},{2,1},{3,2},{4,3},{5,4},{6,5},{7,6},{8,7},{9,8},{10,9},{11,1... | collective-permute-start | bytes 786440 | tf_op jit(solution)/shard_map/ppermute | solution.py:18
  259.3 12.1 %collective-permute-start.15 = (f32[1,4,64,256]{3,2,1,0:T(8,128)}, f32[1,4,64,256]{3,2,1,0:T(8,128)}, u32[]{:S(2)}, u32[]{:S(2)}) collective-permute-start(f32[1,4,64,256]{3,2,1,0:T(8,128)} %get-tuple-element.60), channel_id=1, source_target_pairs={{0,1},{1,2},{2,3},{3,4},{4,5},{5,6},{6,7},{7,8},{8,9},{9,10},{10,1... | collective-permute-start | bytes 786440 | tf_op jit(solution)/shard_map/ppermute | solution.py:15
Sparse Core Ops, SparseCore 0:
  250.8 49.9 all-reduce.9
where the time goes:
time: 313 us; the launch traced here: 310 us
  other arithmetic  148 us (47%)
  starting transfers between devices  77.1 us (25%)
  local copies, waits for them, and re-layouts  32.4 us (10%)
  between operations  26.6 us (8%)
  waiting for transfers between devices  25.7 us (8%)
    ppermute x8, starting transfers between devices, padded(): lax.ppermute(lax.slice_in_dim(block, 0, width, axis=dim), axis, backward)  61.3 us
    add x3, other arithmetic, per_device(): upcoming = 2.0 * current - previous + rate * lap_current  40.6 us
    add x4, other arithmetic, per_device(): earlier = 2.0 * adjoint - later + stencil(extended, scaled)  29.6 us
    mul x4, other arithmetic, per_device(): scaled = rate * adjoint  27.2 us
    unnamed x7, other arithmetic  26 us
    squeeze x1, other arithmetic, per_device(): total = lax.psum(gradient[0], 'shot')  18.2 us
    psum x1, waiting for transfers between devices, per_device(): total = lax.psum(gradient[0], 'shot')  16.3 us
    ppermute x8, starting transfers between devices, padded(): lax.ppermute(lax.slice_in_dim(block, block.shape[dim] - width, None, axis...  15.8 us
  transfers between devices with their start and end apart: 17, of which 3 were waited for; matrix products, arithmetic and copies ran while one was open for 39% of the time, Pallas kernels for 0%

commit v1 on v0

v1 whole, which is shorter than its diff:
```python
import functools

import jax
import jax.numpy as jnp
import numpy as np
from jax import lax
from jax.experimental import pallas as pl
from jax.experimental.pallas import tpu as pltpu
from jax.sharding import PartitionSpec as P

MESH = pl.DeviceIdType.MESH
F32 = jnp.float32
BF16 = jnp.bfloat16

scale = 5040.0
centre = 3.0 * -14350.0
sides = (8064.0, -1008.0, 128.0, -9.0)


def split(values):
    high = values.astype(BF16)
    rest = values - high.astype(F32)
    middle = rest.astype(BF16)
    low = (rest - middle.astype(F32)).astype(BF16)
    return high, middle, low


def band(rows, columns, block):
    row = lax.broadcasted_iota(jnp.int32, (rows, columns), 0)
    column = lax.broadcasted_iota(jnp.int32, (rows, columns), 1)
    away = jnp.abs(row - column)
    result = jnp.zeros((rows, columns), F32)
    for k in range(1, 5):
        result = jnp.where(away == k, sides[k - 1], result)
    if block:
        result = jnp.where(row // block == column // block, result, 0.0)
    return result.astype(BF16)


def kernel(
    doms,
    before_hbm, current_hbm, far_hbm, near_hbm, labels_hbm,
    table, source, wavelet, receivers, residual,
    final_hbm, first_hbm, gradient_hbm,
    ue, u0, u5, se, aa, lap, rate, labels, yzf, yza, stack, along_y, along_z,
    onehot, amounts, inject, spot, grad, near_grad, far_grad, partial, total,
    load_sem, store_sem, send_sem, recv_sem, gsend_sem, grecv_sem,
):
    shot = lax.axis_index("shot")
    dom = lax.axis_index("dom")
    planes, depth, across = u0.shape
    groups = planes // 4
    recs = receivers.shape[1]
    core = lax.rem(shot, 2)
    sibling = shot + 1 - 2 * core
    partner = lax.rem(shot + 2, 4)
    has_low = dom > 0
    has_high = dom < doms - 1

    barrier = pltpu.get_barrier_semaphore()

    def greet(device):
        pl.semaphore_signal(barrier, inc=1, device_id=device, device_id_type=MESH)

    greet({"shot": sibling})
    greet({"shot": partner})

    @pl.when(has_low)
    def _():
        greet({"dom": dom - 1})

    @pl.when(has_high)
    def _():
        greet({"dom": dom + 1})

    loads = [
        pltpu.make_async_copy(labels_hbm, labels, load_sem.at[0]),
        pltpu.make_async_copy(near_hbm.at[0], aa.at[1], load_sem.at[1]),
        pltpu.make_async_copy(current_hbm.at[0], ue.at[0, pl.ds(4, planes)], load_sem.at[2]),
        pltpu.make_async_copy(before_hbm.at[0], u0, load_sem.at[3]),
        pltpu.make_async_copy(far_hbm.at[0], aa.at[0], load_sem.at[4]),
    ]
    for load in loads:
        load.start()

    pl.semaphore_wait(barrier, 2 + jnp.where(has_low, 1, 0) + jnp.where(has_high, 1, 0))

    def to_low(e, source_ref):
        buffer = ue.at[e] if e < 4 else se.at[e - 4]
        return pltpu.make_async_remote_copy(
            source_ref, buffer.at[pl.ds(planes + 4, 4)], send_sem.at[0, e], recv_sem.at[0, e],
            device_id={"dom": dom - 1}, device_id_type=MESH,
        )

    def to_high(e, source_ref):
        buffer = ue.at[e] if e < 4 else se.at[e - 4]
        return pltpu.make_async_remote_copy(
            source_ref, buffer.at[pl.ds(0, 4)], send_sem.at[1, e], recv_sem.at[1, e],
            device_id={"dom": dom + 1}, device_id_type=MESH,
        )

    def low_edge(e):
        if e == 0:
            return current_hbm.at[0, pl.ds(0, 4)]
        return (ue.at[e] if e < 4 else se.at[e - 4]).at[pl.ds(4, 4)]

    def high_edge(e):
        if e == 0:
            return current_hbm.at[0, pl.ds(planes - 4, 4)]
        return (ue.at[e] if e < 4 else se.at[e - 4]).at[pl.ds(planes, 4)]

    def send_low(e):
        @pl.when(has_low)
        def _():
            to_low(e, low_edge(e)).start()

    def send_high(e):
        @pl.when(has_high)
        def _():
            to_high(e, high_edge(e)).start()

    def wait_low(e):
        @pl.when(has_low)
        def _():
            to_high(e, high_edge(e)).wait_recv()

    def wait_high(e):
        @pl.when(has_high)
        def _():
            to_low(e, low_edge(e)).wait_recv()

    send_low(0)
    send_high(0)

    @pl.when(dom == 0)
    def _():
        for e in range(4):
            ue[e, 0:4] = jnp.zeros((4, depth, across), F32)
            se[e, 0:4] = jnp.zeros((4, depth, across), F32)

    @pl.when(dom == doms - 1)
    def _():
        for e in range(4):
            ue[e, planes + 4:planes + 8] = jnp.zeros((4, depth, across), F32)
            se[e, planes + 4:planes + 8] = jnp.zeros((4, depth, across), F32)

    speeds = [table[k] * (1.0 / scale) for k in range(table.shape[0])]
    loads[0].wait()
    loads[1].wait()

    def first_plane(p):
        def rows(i, _):
            r = pl.ds(pl.multiple_of(i * 16, 16), 16)
            region = labels[p, r, :]
            speed = jnp.full(region.shape, speeds[0], F32)
            for k in range(1, len(speeds)):
                speed = jnp.where(region == k, speeds[k], speed)
            rate[p, r, :] = speed
            se[0, p + 4, r, :] = speed * aa[1, p, r, :]
            return 0

        lax.fori_loop(0, depth // 16, rows, 0)

    def first_group(base):
        lax.fori_loop(0, 4, lambda j, c: (first_plane(base + j), c)[1], 0)

    first_group(0)
    send_low(4)
    first_group(planes - 4)
    send_high(4)
    lax.fori_loop(4, planes - 4, lambda p, c: (first_plane(p), c)[1], 0)

    along_y[...] = band(across, across, 0)
    plane_band = band(4 * depth, 4 * depth, depth)
    for k in range(3):
        along_z[:, k * 4 * depth:(k + 1) * 4 * depth] = plane_band

    row = lax.broadcasted_iota(jnp.int32, (depth, across), 0)
    column = lax.broadcasted_iota(jnp.int32, (depth, across), 1)
    spot[...] = jnp.where((row == source[0, 1]) & (column == source[0, 2]), 1.0, 0.0).astype(F32)
    source_plane = source[0, 0] - dom * planes

    def across_stage(ext, out):
        def group(g, _):
            for q in range(4):
                def rows(i, _, q=q):
                    at = pl.multiple_of(i * 16, 16)
                    parts = split(ext[4 + 4 * g + q, pl.ds(at, 16), :])
                    for k in range(3):
                        stack[pl.ds(pl.multiple_of(at + (4 * k + q) * depth, 16), 16), :] = parts[k]
                    return 0

                lax.fori_loop(0, depth // 16, rows, 0, unroll=True)
            size = 4 * depth
            in_y = jnp.dot(stack[...], along_y[...], preferred_element_type=F32)
            in_z = jnp.dot(along_z[...], stack[...], preferred_element_type=F32)
            both = (in_y[2 * size:] + in_y[size:2 * size]) + in_y[:size] + in_z
            out[pl.ds(4 * g, 4)] = both.reshape(4, depth, across)
            return 0

        lax.fori_loop(0, groups, group, 0)

    def laplace(planes_of, j, rest):
        result = rest + centre * planes_of[j + 4]
        for k in range(1, 5):
            result = result + sides[k - 1] * (planes_of[j + 4 + k] + planes_of[j + 4 - k])
        return result

    def forward_group(n, g):
        pulses = [jnp.where(source_plane == 4 * g + j, wavelet[0, n], 0.0) for j in range(4)]

        def rows(i, _):
            r = pl.ds(pl.multiple_of(i * 8, 8), 8)
            window = [ue[n, 4 * g + q, r, :] for q in range(12)]
            for j in range(4):
                p = 4 * g + j
                curve = laplace(window, j, yzf[p, r, :])
                lap[n, p, r, :] = curve
                previous = u0[p, r, :] if n == 0 else ue[n - 1, p + 4, r, :]
                upcoming = 2.0 * window[j + 4] - previous + rate[p, r, :] * curve
                upcoming = upcoming + pulses[j] * spot[r, :]
                if n == 3:
                    u5[p, r, :] = upcoming
                else:
                    ue[n + 1, p + 4, r, :] = upcoming
            return 0

        lax.fori_loop(0, depth // 8, rows, 0)

    def adjoint_group(m, g):
        def rows(i, _):
            r = pl.ds(pl.multiple_of(i * 8, 8), 8)
            window = [se[m, 4 * g + q, r, :] for q in range(12)]
            for j in range(4):
                p = 4 * g + j
                curve = laplace(window, j, yza[p, r, :])
                earlier = 2.0 * aa[m + 1, p, r, :] - aa[m, p, r, :] + curve + inject[3 - m, p, r, :]
                aa[m + 2, p, r, :] = earlier
                if m < 3:
                    se[m + 1, p + 4, r, :] = rate[p, r, :] * earlier
            return 0

        lax.fori_loop(0, depth // 8, rows, 0)

    def middle(one, n):
        lax.fori_loop(1, groups - 1, lambda g, c: (one(n, g), c)[1], 0)

    cell = (receivers[0:1, :] - dom * planes) * depth + receivers[1:2, :]

    def onehot_rows(i, _):
        at = pl.multiple_of(i * 16, 16)
        here = lax.broadcasted_iota(jnp.int32, (16, recs), 0) + at
        onehot[pl.ds(at, 16), :] = jnp.where(here == cell, 1.0, 0.0).astype(BF16)
        return 0

    def inject_step(n, _):
        value = residual[pl.ds(n, 1), :]
        parts = [part.astype(F32) for part in split(value)]

        def columns(i, _):
            at = pl.multiple_of(i * 16, 16)
            here = lax.broadcasted_iota(jnp.int32, (16, recs), 0) + at == receivers[2:3, :]
            for k in range(3):
                amounts[pl.ds(pl.multiple_of(at + k * across, 16), 16), :] = jnp.where(here, parts[k], 0.0).astype(BF16)
            return 0

        lax.fori_loop(0, across // 16, columns, 0)

        def group(g, _):
            rows = pl.ds(pl.multiple_of(g * 4 * depth, 4 * depth), 4 * depth)
            spread = lax.dot_general(
                onehot[rows, :], amounts[...], (((1,), (1,)), ((), ())), preferred_element_type=F32
            )
            both = (spread[:, 2 * across:] + spread[:, across:2 * across]) + spread[:, :across]
            inject[n, pl.ds(4 * g, 4)] = both.reshape(4, depth, across)
            return 0

        lax.fori_loop(0, groups, group, 0)
        return 0

    def combine(p, _):
        def rows(i, _):
            r = pl.ds(pl.multiple_of(i * 16, 16), 16)
            value = aa[1, p, r, :] * lap[3, p, r, :]
            for n in (2, 1, 0):
                value = value + aa[4 - n, p, r, :] * lap[n, p, r, :]
            grad[p, r, :] = value
            return 0

        lax.fori_loop(0, depth // 16, rows, 0)
        return 0

    mine = (4 + 4 * core, (planes - 4) * core)
    other = (8 - 4 * core, (planes - 4) * (1 - core))

    def to_sibling(c):
        return pltpu.make_async_remote_copy(
            grad.at[pl.ds(other[c], 4)], near_grad.at[c], gsend_sem.at[0, c], grecv_sem.at[0, c],
            device_id={"shot": sibling}, device_id_type=MESH,
        )

    def to_partner(c):
        return pltpu.make_async_remote_copy(
            partial.at[c], far_grad.at[c], gsend_sem.at[1, c], grecv_sem.at[1, c],
            device_id={"shot": partner}, device_id_type=MESH,
        )

    def total_to_sibling(c):
        return pltpu.make_async_remote_copy(
            total.at[c], gradient_hbm.at[pl.ds(mine[c], 4)], gsend_sem.at[2, c], grecv_sem.at[2, c],
            device_id={"shot": sibling}, device_id_type=MESH,
        )

    def total_home(c):
        return pltpu.make_async_copy(total.at[c], gradient_hbm.at[pl.ds(mine[c], 4)], store_sem.at[c])

    def sum_near(c):
        to_sibling(c).wait_recv()

        def one(j, _):
            partial[c, j] = grad[mine[c] + j] + near_grad[c, j]
            return 0

        lax.fori_loop(0, 4, one, 0)
        to_partner(c).start()

    def sum_far(c):
        to_partner(c).wait_recv()

        def one(j, _):
            total[c, j] = (partial[c, j] + far_grad[c, j]) * (1.0 / scale)
            return 0

        lax.fori_loop(0, 4, one, 0)
        total_to_sibling(c).start()
        total_home(c).start()

    loads[2].wait()
    across_stage(ue.at[0], yzf)
    loads[3].wait()
    middle(forward_group, 0)
    lax.fori_loop(0, planes * depth // 16, onehot_rows, 0)
    lax.fori_loop(3, 4, inject_step, 0)

    stores = [
        pltpu.make_async_copy(u5, final_hbm.at[0], store_sem.at[2]),
        pltpu.make_async_copy(aa.at[5], first_hbm.at[0], store_sem.at[3]),
    ]

    for n in range(4):
        wait_low(n)
        forward_group(n, 0)
        if n < 3:
            send_low(n + 1)
        wait_high(n)
        forward_group(n, groups - 1)
        if n < 3:
            send_high(n + 1)
            across_stage(ue.at[n + 1], yzf)
            middle(forward_group, n + 1)
        if n == 0:
            loads[4].wait()
            across_stage(se.at[0], yza)
            middle(adjoint_group, 0)
        if n == 2:
            lax.fori_loop(4, planes - 4, combine, 0)
            to_sibling(0).start()
        if n == 3:
            lax.fori_loop(0, 4, combine, 0)
            lax.fori_loop(planes - 4, planes, combine, 0)
            to_sibling(1).start()
            stores[0].start()
            sum_far(0)
            sum_near(1)
        wait_low(n + 4)
        adjoint_group(n, 0)
        if n < 3:
            send_low(n + 5)
        wait_high(n + 4)
        adjoint_group(n, groups - 1)
        if n < 3:
            send_high(n + 5)
        if n == 2:
            sum_near(0)
        if n == 0:
            lax.fori_loop(0, 3, inject_step, 0)
        if n < 3:
            across_stage(se.at[n + 1], yza)
            middle(adjoint_group, n + 1)
    stores[1].start()
    sum_far(1)

    for c in range(2):
        total_to_sibling(c).wait_recv()
    for e in range(8):
        @pl.when(has_low)
        def _():
            to_low(e, low_edge(e)).wait_send()

        @pl.when(has_high)
        def _():
            to_high(e, high_edge(e)).wait_send()
    for c in range(2):
        to_sibling(c).wait_send()
        to_partner(c).wait_send()
        total_to_sibling(c).wait_send()
        total_home(c).wait()
    for store in stores:
        store.wait()


def per_device(
    doms, wave_before, wave_current, adjoint_far, adjoint_near, labels, table,
    source_index, wavelet, receiver_index, residual,
):
    block = wave_current.shape
    planes, depth, across = labels.shape
    recs = receiver_index.shape[1]
    field = (planes, depth, across)
    extended = (4, planes + 8, depth, across)
    whole = pl.BlockSpec(memory_space=pl.ANY)
    scalars = pl.BlockSpec(memory_space=pltpu.SMEM)
    vectors = pl.BlockSpec(memory_space=pltpu.VMEM)
    return pl.pallas_call(
        functools.partial(kernel, doms),
        out_shape=(
            jax.ShapeDtypeStruct(block, F32),
            jax.ShapeDtypeStruct(block, F32),
            jax.ShapeDtypeStruct(field, F32),
        ),
        in_specs=[whole] * 5 + [scalars] * 3 + [vectors] * 2,
        out_specs=(whole, whole, whole),
        scratch_shapes=[
            pltpu.VMEM(extended, F32),
            pltpu.VMEM(field, F32),
            pltpu.VMEM(field, F32),
            pltpu.VMEM(extended, F32),
            pltpu.VMEM((6,) + field, F32),
            pltpu.VMEM((4,) + field, F32),
            pltpu.VMEM(field, F32),
            pltpu.VMEM(field, jnp.int32),
            pltpu.VMEM(field, F32),
            pltpu.VMEM(field, F32),
            pltpu.VMEM((12 * depth, across), BF16),
            pltpu.VMEM((across, across), BF16),
            pltpu.VMEM((4 * depth, 12 * depth), BF16),
            pltpu.VMEM((planes * depth, recs), BF16),
            pltpu.VMEM((3 * across, recs), BF16),
            pltpu.VMEM((4,) + field, F32),
            pltpu.VMEM((depth, across), F32),
            pltpu.VMEM(field, F32),
            pltpu.VMEM((2, 4, depth, across), F32),
            pltpu.VMEM((2, 4, depth, across), F32),
            pltpu.VMEM((2, 4, depth, across), F32),
            pltpu.VMEM((2, 4, depth, across), F32),
            pltpu.SemaphoreType.DMA((5,)),
            pltpu.SemaphoreType.DMA((4,)),
            pltpu.SemaphoreType.DMA((2, 8)),
            pltpu.SemaphoreType.DMA((2, 8)),
            pltpu.SemaphoreType.DMA((3, 2)),
            pltpu.SemaphoreType.DMA((3, 2)),
        ],
        compiler_params=pltpu.CompilerParams(
            collective_id=0, has_side_effects=True, vmem_limit_bytes=56 << 20
        ),
        name="window",
    )(
        wave_before, wave_current, adjoint_far, adjoint_near, labels, table,
        source_index, wavelet, jnp.transpose(receiver_index[0]), residual[0],
    )


def solution(mesh):
    fields = P("shot", "dom", None, None)
    return jax.shard_map(
        functools.partial(per_device, mesh.shape["dom"]),
        mesh=mesh,
        in_specs=(
            fields, fields, fields, fields, P("dom", None, None), P(),
            P("shot", None), P("shot", None), P("shot", None, None), P("shot", None, None),
        ),
        out_specs=(fields, fields, P("dom", None, None)),
        check_vma=False,
    )
```

time: 313 us -> 82.1 us (0.26)
  other arithmetic: 148 us -> 0 us
  starting transfers between devices: 77.1 us -> 0 us
  Pallas kernels: 0 us -> 73.7 us
  local copies, waits for them, and re-layouts: 32.4 us -> 6.27 us
  between operations: 26.6 us -> 0.65 us
  waiting for transfers between devices: 25.7 us -> 0 us
    ppermute x16 -> x0, starting transfers between devices: 77.1 us -> none  [the longest x8 61.3 us: padded(): lax.ppermute(lax.slice_in_dim(block, 0, width, axis=dim), axis, backward)]
    add x11 -> x0, other arithmetic: 76 us -> none  [the longest x3 40.6 us: per_device(): upcoming = 2.0 * current - previous + rate * lap_current]
    pallas_call x0 -> x1, Pallas kernels: none -> 73.7 us  [per_device(): pl.pallas_call(functools.partial(kernel, doms), out_shape=(jax.ShapeDtype...]
    mul x4 -> x0, other arithmetic: 27.2 us -> none  [per_device(): scaled = rate * adjoint]
    unnamed x7 -> x0, other arithmetic: 26 us -> none
    squeeze x1 -> x0, other arithmetic: 18.2 us -> none  [per_device(): total = lax.psum(gradient[0], 'shot')]
    psum x1 -> x0, waiting for transfers between devices: 16.3 us -> none  [per_device(): total = lax.psum(gradient[0], 'shot')]
    slice x12 -> x0, local copies, waits for them, and re-layouts: 13 us -> none  [the longest x8 10.1 us: padded(): lax.slice_in_dim(block, 0, width, axis=dim)]
  transfers between devices with their start and end apart: 17 -> 0, of which waited for: 3 -> 0; matrix products, arithmetic and copies ran while one was open for 39% -> 0% of each run, Pallas kernels for 0% -> 0%
where the time goes in v1:
time: 82.1 us; the launch traced here: 80.7 us
  Pallas kernels  73.7 us (90%)
  local copies, waits for them, and re-layouts  6.27 us (8%)
    pallas_call x1, Pallas kernels, per_device(): pl.pallas_call(functools.partial(kernel, doms), out_shape=(jax.ShapeDtype...  73.7 us
    unnamed x8, local copies, waits for them, and re-layouts  6.27 us

profile of v1, /device:TPU:7, one launch (start us, length us, event | category | flops | bytes accessed | tf_op | source)
XLA Modules:
  0.0 80.7 jit_solution(6067285381050556651)
XLA Ops:
  0.6 1.3 %copy.15 = s32[1,1024,3]{1,2,0:T(4,128)} copy(s32[1,1024,3]{1,0,2:T(1,128)} %param.18) | data formatting | bytes 24576
  1.9 73.7 %window.1 = (f32[1,16,64,256]{3,2,1,0:T(8,128)}, f32[1,16,64,256]{3,2,1,0:T(8,128)}, f32[16,64,256]{2,1,0:T(8,128)}) custom-call(f32[1,16,64,256]{3,2,1,0:T(8,128)} %before_hbm.1, f32[1,16,64,256]{3,2,1,0:T(8,128)} %current_hbm.1, f32[1,16,64,256]{3,2,1,0:T(8,128)} %far_hbm.1, f32[1,16,64,256]{3,2,1,0:T(8,128)} %near_hbm.1, s32[16,64,256]{2,1,0:T(8,128)} %labels_hbm.1, ...), custom_call_target="tpu_custom_call" | custom-call | tf_op jit(solution)/shard_map/window/pallas_call | solution.py:424
  75.7 0.0 copy-start.1
  75.7 2.4 %copy.19 = f32[1,16,64,256]{3,2,1,0:T(8,128)} copy(f32[1,16,64,256]{3,2,1,0:T(8,128)} %get-tuple-element.6) | data formatting | bytes 2097152
  78.1 0.0 copy-done.1
  78.1 0.0 copy-start
  78.1 1.0 %copy.20 = f32[1,16,64,256]{3,2,1,0:T(8,128)} copy(f32[1,16,64,256]{3,2,1,0:T(8,128)S(1)} %copy-done.1) | data formatting | bytes 2097152
  79.0 0.6 copy-done
  79.7 1.0 %copy.21 = f32[16,64,256]{2,1,0:T(8,128)} copy(f32[16,64,256]{2,1,0:T(8,128)S(1)} %copy-done) | data formatting | bytes 2097152
Async XLA Ops:
  75.7 2.4 %copy-start.1 = (f32[1,16,64,256]{3,2,1,0:T(8,128)S(1)}, f32[1,16,64,256]{3,2,1,0:T(8,128)}, u32[]{:S(2)}) copy-start(f32[1,16,64,256]{3,2,1,0:T(8,128)} %get-tuple-element.7) | copy-start | bytes 3145732
  78.1 1.6 %copy-start = (f32[16,64,256]{2,1,0:T(8,128)S(1)}, f32[16,64,256]{2,1,0:T(8,128)}, u32[]{:S(2)}) copy-start(f32[16,64,256]{2,1,0:T(8,128)} %get-tuple-element.8) | copy-start | bytes 3145732

commit v2 on v1

--- a/solution.py
+++ b/solution.py
@@ -11,6 +11,8 @@
 MESH = pl.DeviceIdType.MESH
 F32 = jnp.float32
 BF16 = jnp.bfloat16
+
+ring = 8
 
 scale = 5040.0
 centre = 3.0 * -14350.0
@@ -41,19 +43,24 @@
     doms,
     before_hbm, current_hbm, far_hbm, near_hbm, labels_hbm,
     table, source, wavelet, receivers, residual,
-    final_hbm, first_hbm, gradient_hbm,
-    ue, u0, u5, se, aa, lap, rate, labels, yzf, yza, stack, along_y, along_z,
-    onehot, amounts, inject, spot, grad, near_grad, far_grad, partial, total,
-    load_sem, store_sem, send_sem, recv_sem, gsend_sem, grecv_sem,
+    final, first, gradient,
+    ue, u0, se, aa, lap, rate, labels, yzf, yza, stack, along_y, along_z,
+    onehot, amounts, inject, spot, grad, near_grad, far_grad, partial, passing,
+    load_sem, send_sem, recv_sem, gsend_sem, grecv_sem, psend_sem, precv_sem,
 ):
     shot = lax.axis_index("shot")
     dom = lax.axis_index("dom")
     planes, depth, across = u0.shape
     groups = planes // 4
-    recs = receivers.shape[1]
+    recs = receivers.shape[2]
     core = lax.rem(shot, 2)
     sibling = shot + 1 - 2 * core
     partner = lax.rem(shot + 2, 4)
+    place = lax.rem(dom, ring)
+    at_end = (place == 0) | (place == ring - 1)
+    passes = (place == 1) | (place == ring - 2)
+    inside = jnp.where(place == 0, dom + 1, dom - 1)
+    outside = jnp.where(place == 1, dom - 1, dom + 1)
     has_low = dom > 0
     has_high = dom < doms - 1
 
@@ -64,6 +71,14 @@
 
     greet({"shot": sibling})
     greet({"shot": partner})
+
+    @pl.when(at_end)
+    def _():
+        greet({"shot": partner, "dom": inside})
+
+    @pl.when(passes)
+    def _():
+        greet({"shot": partner, "dom": outside})
 
     @pl.when(has_low)
     def _():
@@ -83,7 +98,8 @@
     for load in loads:
         load.start()
 
-    pl.semaphore_wait(barrier, 2 + jnp.where(has_low, 1, 0) + jnp.where(has_high, 1, 0))
+    peers = 2 + jnp.where(at_end | passes, 1, 0) + jnp.where(has_low, 1, 0) + jnp.where(has_high, 1, 0)
+    pl.semaphore_wait(barrier, peers)
 
     def to_low(e, source_ref):
         buffer = ue.at[e] if e < 4 else se.at[e - 4]
@@ -220,7 +236,7 @@
                 upcoming = 2.0 * window[j + 4] - previous + rate[p, r, :] * curve
                 upcoming = upcoming + pulses[j] * spot[r, :]
                 if n == 3:
-                    u5[p, r, :] = upcoming
+                    final[0, p, r, :] = upcoming
                 else:
                     ue[n + 1, p + 4, r, :] = upcoming
             return 0
@@ -235,8 +251,10 @@
                 p = 4 * g + j
                 curve = laplace(window, j, yza[p, r, :])
                 earlier = 2.0 * aa[m + 1, p, r, :] - aa[m, p, r, :] + curve + inject[3 - m, p, r, :]
-                aa[m + 2, p, r, :] = earlier
-                if m < 3:
+                if m == 3:
+                    first[0, p, r, :] = earlier
+                else:
+                    aa[m + 2, p, r, :] = earlier
                     se[m + 1, p + 4, r, :] = rate[p, r, :] * earlier
             return 0
 
@@ -245,7 +263,7 @@
     def middle(one, n):
         lax.fori_loop(1, groups - 1, lambda g, c: (one(n, g), c)[1], 0)
 
-    cell = (receivers[0:1, :] - dom * planes) * depth + receivers[1:2, :]
+    cell = (receivers[0] - dom * planes) * depth + receivers[1]
 
     def onehot_rows(i, _):
         at = pl.multiple_of(i * 16, 16)
@@ -253,13 +271,15 @@
         onehot[pl.ds(at, 16), :] = jnp.where(here == cell, 1.0, 0.0).astype(BF16)
         return 0
 
+    lax.fori_loop(0, planes * depth // 16, onehot_rows, 0)
+
     def inject_step(n, _):
         value = residual[pl.ds(n, 1), :]
         parts = [part.astype(F32) for part in split(value)]
 
         def columns(i, _):
             at = pl.multiple_of(i * 16, 16)
-            here = lax.broadcasted_iota(jnp.int32, (16, recs), 0) + at == receivers[2:3, :]
+            here = lax.broadcasted_iota(jnp.int32, (16, recs), 0) + at == receivers[2]
             for k in range(3):
                 amounts[pl.ds(pl.multiple_of(at + k * across, 16), 16), :] = jnp.where(here, parts[k], 0.0).astype(BF16)
             return 0
@@ -305,14 +325,23 @@
             device_id={"shot": partner}, device_id_type=MESH,
         )
 
+    def to_passer():
+        return pltpu.make_async_remote_copy(
+            partial.at[0], passing, psend_sem.at[0], precv_sem.at[0],
+            device_id={"shot": partner, "dom": inside}, device_id_type=MESH,
+        )
+
+    def pass_on():
+        return pltpu.make_async_remote_copy(
+            passing, far_grad.at[0], psend_sem.at[1], precv_sem.at[1],
+            device_id={"dom": outside}, device_id_type=MESH,
+        )
+
     def total_to_sibling(c):
         return pltpu.make_async_remote_copy(
-            total.at[c], gradient_hbm.at[pl.ds(mine[c], 4)], gsend_sem.at[2, c], grecv_sem.at[2, c],
+            gradient.at[pl.ds(mine[c], 4)], gradient.at[pl.ds(mine[c], 4)], gsend_sem.at[2, c], grecv_sem.at[2, c],
             device_id={"shot": sibling}, device_id_type=MESH,
         )
-
-    def total_home(c):
-        return pltpu.make_async_copy(total.at[c], gradient_hbm.at[pl.ds(mine[c], 4)], store_sem.at[c])
 
     def sum_near(c):
         to_sibling(c).wait_recv()
@@ -322,30 +351,40 @@
             return 0
 
         lax.fori_loop(0, 4, one, 0)
-        to_partner(c).start()
+        if c == 1:
+            to_partner(c).start()
+        else:
+            @pl.when(at_end)
+            def _():
+                to_passer().start()
+
+            @pl.when(jnp.logical_not(at_end))
+            def _():
+                to_partner(c).start()
 
     def sum_far(c):
-        to_partner(c).wait_recv()
+        if c == 1:
+            to_partner(c).wait_recv()
+        else:
+            @pl.when(at_end)
+            def _():
+                pass_on().wait_recv()
+
+            @pl.when(jnp.logical_not(at_end))
+            def _():
+                to_partner(c).wait_recv()
 
         def one(j, _):
-            total[c, j] = (partial[c, j] + far_grad[c, j]) * (1.0 / scale)
+            gradient[mine[c] + j] = (partial[c, j] + far_grad[c, j]) * (1.0 / scale)
             return 0
 
         lax.fori_loop(0, 4, one, 0)
         total_to_sibling(c).start()
-        total_home(c).start()
 
     loads[2].wait()
     across_stage(ue.at[0], yzf)
     loads[3].wait()
     middle(forward_group, 0)
-    lax.fori_loop(0, planes * depth // 16, onehot_rows, 0)
-    lax.fori_loop(3, 4, inject_step, 0)
-
-    stores = [
-        pltpu.make_async_copy(u5, final_hbm.at[0], store_sem.at[2]),
-        pltpu.make_async_copy(aa.at[5], first_hbm.at[0], store_sem.at[3]),
-    ]
 
     for n in range(4):
         wait_low(n)
@@ -360,18 +399,26 @@
             middle(forward_group, n + 1)
         if n == 0:
             loads[4].wait()
+            lax.fori_loop(3, 4, inject_step, 0)
             across_stage(se.at[0], yza)
             middle(adjoint_group, 0)
         if n == 2:
             lax.fori_loop(4, planes - 4, combine, 0)
             to_sibling(0).start()
+            sum_near(0)
         if n == 3:
             lax.fori_loop(0, 4, combine, 0)
             lax.fori_loop(planes - 4, planes, combine, 0)
             to_sibling(1).start()
-            stores[0].start()
-            sum_far(0)
+
+            @pl.when(passes)
+            def _():
+                to_passer().wait_recv()
+                pass_on().start()
+
             sum_near(1)
+        if n == 1:
+            lax.fori_loop(1, 2, inject_step, 0)
         wait_low(n + 4)
         adjoint_group(n, 0)
         if n < 3:
@@ -380,14 +427,12 @@
         adjoint_group(n, groups - 1)
         if n < 3:
             send_high(n + 5)
-        if n == 2:
-            sum_near(0)
-        if n == 0:
-            lax.fori_loop(0, 3, inject_step, 0)
+        if n < 2:
+            lax.fori_loop(2 - 2 * n, 3 - 2 * n, inject_step, 0)
         if n < 3:
             across_stage(se.at[n + 1], yza)
             middle(adjoint_group, n + 1)
-    stores[1].start()
+    sum_far(0)
     sum_far(1)
 
     for c in range(2):
@@ -402,11 +447,21 @@
             to_high(e, high_edge(e)).wait_send()
     for c in range(2):
         to_sibling(c).wait_send()
-        to_partner(c).wait_send()
         total_to_sibling(c).wait_send()
-        total_home(c).wait()
-    for store in stores:
-        store.wait()
+
+    @pl.when(at_end)
+    def _():
+        to_passer().wait_send()
+
+    @pl.when(passes)
+    def _():
+        pass_on().wait_send()
+
+    @pl.when(jnp.logical_not(at_end))
+    def _():
+        to_partner(0).wait_send()
+
+    to_partner(1).wait_send()
 
 
 def per_device(
@@ -418,24 +473,23 @@
     recs = receiver_index.shape[1]
     field = (planes, depth, across)
     extended = (4, planes + 8, depth, across)
-    whole = pl.BlockSpec(memory_space=pl.ANY)
+    whole = pl.BlockSpec(memory_space=pltpu.HBM)
     scalars = pl.BlockSpec(memory_space=pltpu.SMEM)
     vectors = pl.BlockSpec(memory_space=pltpu.VMEM)
     return pl.pallas_call(
         functools.partial(kernel, doms),
         out_shape=(
-            jax.ShapeDtypeStruct(block, F32),
-            jax.ShapeDtypeStruct(block, F32),
-            jax.ShapeDtypeStruct(field, F32),
+            pltpu.VMEM(block, F32),
+            pltpu.VMEM(block, F32),
+            pltpu.VMEM(field, F32),
         ),
         in_specs=[whole] * 5 + [scalars] * 3 + [vectors] * 2,
-        out_specs=(whole, whole, whole),
+        out_specs=(vectors, vectors, vectors),
         scratch_shapes=[
             pltpu.VMEM(extended, F32),
             pltpu.VMEM(field, F32),
-            pltpu.VMEM(field, F32),
             pltpu.VMEM(extended, F32),
-            pltpu.VMEM((6,) + field, F32),
+            pltpu.VMEM((5,) + field, F32),
             pltpu.VMEM((4,) + field, F32),
             pltpu.VMEM(field, F32),
             pltpu.VMEM(field, jnp.int32),
@@ -452,21 +506,22 @@
             pltpu.VMEM((2, 4, depth, across), F32),
             pltpu.VMEM((2, 4, depth, across), F32),
             pltpu.VMEM((2, 4, depth, across), F32),
-            pltpu.VMEM((2, 4, depth, across), F32),
+            pltpu.VMEM((4, depth, across), F32),
             pltpu.SemaphoreType.DMA((5,)),
-            pltpu.SemaphoreType.DMA((4,)),
             pltpu.SemaphoreType.DMA((2, 8)),
             pltpu.SemaphoreType.DMA((2, 8)),
             pltpu.SemaphoreType.DMA((3, 2)),
             pltpu.SemaphoreType.DMA((3, 2)),
+            pltpu.SemaphoreType.DMA((2,)),
+            pltpu.SemaphoreType.DMA((2,)),
         ],
         compiler_params=pltpu.CompilerParams(
-            collective_id=0, has_side_effects=True, vmem_limit_bytes=56 << 20
+            collective_id=0, has_side_effects=True, vmem_limit_bytes=60 << 20
         ),
         name="window",
     )(
         wave_before, wave_current, adjoint_far, adjoint_near, labels, table,
-        source_index, wavelet, jnp.transpose(receiver_index[0]), residual[0],
+        source_index, wavelet, jnp.transpose(receiver_index, (2, 0, 1)), residual[0],
     )
 
 

time: 82.1 us -> 69.3 us (0.84); the launches traced: 80.7 us -> 69.1 us
  Pallas kernels: 73.7 us -> 65.6 us
  local copies, waits for them, and re-layouts: 6.27 us -> 2.91 us
    pallas_call x1, Pallas kernels: 73.7 us -> 65.6 us  [per_device(): pl.pallas_call(functools.partial(kernel, doms), out_shape=(pltpu.VMEM(blo...]
    unnamed x8 -> x3, local copies, waits for them, and re-layouts: 6.27 us -> 2.91 us
where the time goes in v2:
time: 69.3 us; the launch traced here: 69.1 us
  Pallas kernels  65.6 us (95%)
  local copies, waits for them, and re-layouts  2.91 us (4%)
    pallas_call x1, Pallas kernels, per_device(): pl.pallas_call(functools.partial(kernel, doms), out_shape=(pltpu.VMEM(blo...  65.6 us
    unnamed x3, local copies, waits for them, and re-layouts  2.91 us

profile of v2, /device:TPU:7, one launch (start us, length us, event | category | flops | bytes accessed | tf_op | source)
XLA Modules:
  0.0 69.1 jit_solution(17673173425528870101)
XLA Ops:
  0.6 65.6 %window.1 = (f32[1,16,64,256]{3,2,1,0:T(8,128)S(1)}, f32[1,16,64,256]{3,2,1,0:T(8,128)S(1)}, f32[16,64,256]{2,1,0:T(8,128)S(1)}) custom-call(f32[1,16,64,256]{3,2,1,0:T(8,128)} %before_hbm.1, f32[1,16,64,256]{3,2,1,0:T(8,128)} %current_hbm.1, f32[1,16,64,256]{3,2,1,0:T(8,128)} %far_hbm.1, f32[1,16,64,256]{3,2,1,0:T(8,128)} %near_hbm.1, ...), custom_call_target="tpu_custom_call" | custom-call | tf_op jit(solution)/shard_map/window/pallas_call | solution.py:479
  66.2 1.0 %copy.16 = f32[1,16,64,256]{3,2,1,0:T(8,128)} copy(f32[1,16,64,256]{3,2,1,0:T(8,128)S(1)} %get-tuple-element.3) | data formatting | bytes 2097152
  67.2 1.0 %copy.17 = f32[1,16,64,256]{3,2,1,0:T(8,128)} copy(f32[1,16,64,256]{3,2,1,0:T(8,128)S(1)} %get-tuple-element.4) | data formatting | bytes 2097152
  68.1 1.0 %copy.18 = f32[16,64,256]{2,1,0:T(8,128)} copy(f32[16,64,256]{2,1,0:T(8,128)S(1)} %get-tuple-element.5) | data formatting | bytes 2097152

commit v3 on v2

--- a/solution.py
+++ b/solution.py
@@ -42,11 +42,11 @@
 def kernel(
     doms,
     before_hbm, current_hbm, far_hbm, near_hbm, labels_hbm,
-    table, source, wavelet, receivers, residual,
+    table_hbm, source_hbm, wavelet_hbm, receivers_hbm, residual_hbm,
     final, first, gradient,
-    ue, u0, se, aa, lap, rate, labels, yzf, yza, stack, along_y, along_z,
+    table, source, wavelet, receivers, residual, ue, u0, se, aa, lap, rate, labels, yzf, yza, stack, along_y, along_z,
     onehot, amounts, inject, spot, grad, near_grad, far_grad, partial, passing,
-    load_sem, send_sem, recv_sem, gsend_sem, grecv_sem, psend_sem, precv_sem,
+    load_sem, send_sem, recv_sem, gsend_sem, grecv_sem,
 ):
     shot = lax.axis_index("shot")
     dom = lax.axis_index("dom")
@@ -94,9 +94,14 @@
         pltpu.make_async_copy(current_hbm.at[0], ue.at[0, pl.ds(4, planes)], load_sem.at[2]),
         pltpu.make_async_copy(before_hbm.at[0], u0, load_sem.at[3]),
         pltpu.make_async_copy(far_hbm.at[0], aa.at[0], load_sem.at[4]),
+        pltpu.make_async_copy(table_hbm, table, load_sem.at[5]),
+        pltpu.make_async_copy(source_hbm, source, load_sem.at[6]),
+        pltpu.make_async_copy(wavelet_hbm, wavelet, load_sem.at[7]),
+        pltpu.make_async_copy(receivers_hbm, receivers, load_sem.at[8]),
+        pltpu.make_async_copy(residual_hbm, residual, load_sem.at[9]),
     ]
-    for load in loads:
-        load.start()
+    for k in (5, 0, 1, 2, 3, 6, 7, 8, 9, 4):
+        loads[k].start()
 
     peers = 2 + jnp.where(at_end | passes, 1, 0) + jnp.where(has_low, 1, 0) + jnp.where(has_high, 1, 0)
     pl.semaphore_wait(barrier, peers)
@@ -160,6 +165,7 @@
             ue[e, planes + 4:planes + 8] = jnp.zeros((4, depth, across), F32)
             se[e, planes + 4:planes + 8] = jnp.zeros((4, depth, across), F32)
 
+    loads[5].wait()
     speeds = [table[k] * (1.0 / scale) for k in range(table.shape[0])]
     loads[0].wait()
     loads[1].wait()
@@ -191,6 +197,8 @@
     for k in range(3):
         along_z[:, k * 4 * depth:(k + 1) * 4 * depth] = plane_band
 
+    for k in range(6, 10):
+        loads[k].wait()
     row = lax.broadcasted_iota(jnp.int32, (depth, across), 0)
     column = lax.broadcasted_iota(jnp.int32, (depth, across), 1)
     spot[...] = jnp.where((row == source[0, 1]) & (column == source[0, 2]), 1.0, 0.0).astype(F32)
@@ -231,7 +239,10 @@
             for j in range(4):
                 p = 4 * g + j
                 curve = laplace(window, j, yzf[p, r, :])
-                lap[n, p, r, :] = curve
+                if n == 3:
+                    grad[p, r, :] = grad[p, r, :] + aa[1, p, r, :] * curve
+                else:
+                    lap[n, p, r, :] = curve
                 previous = u0[p, r, :] if n == 0 else ue[n - 1, p + 4, r, :]
                 upcoming = 2.0 * window[j + 4] - previous + rate[p, r, :] * curve
                 upcoming = upcoming + pulses[j] * spot[r, :]
@@ -301,8 +312,8 @@
     def combine(p, _):
         def rows(i, _):
             r = pl.ds(pl.multiple_of(i * 16, 16), 16)
-            value = aa[1, p, r, :] * lap[3, p, r, :]
-            for n in (2, 1, 0):
+            value = aa[2, p, r, :] * lap[2, p, r, :]
+            for n in (1, 0):
                 value = value + aa[4 - n, p, r, :] * lap[n, p, r, :]
             grad[p, r, :] = value
             return 0
@@ -310,76 +321,85 @@
         lax.fori_loop(0, depth // 16, rows, 0)
         return 0
 
-    mine = (4 + 4 * core, (planes - 4) * core)
-    other = (8 - 4 * core, (planes - 4) * (1 - core))
-
-    def to_sibling(c):
+    mine, other = 4 + 4 * core, 8 - 4 * core
+    mine_edge, other_edge = (planes - 4) * core, (planes - 4) * (1 - core)
+
+    def gradient_copy(phase, chunk, source_ref, target_ref, device):
         return pltpu.make_async_remote_copy(
-            grad.at[pl.ds(other[c], 4)], near_grad.at[c], gsend_sem.at[0, c], grecv_sem.at[0, c],
-            device_id={"shot": sibling}, device_id_type=MESH,
+            source_ref, target_ref, gsend_sem.at[phase, chunk], grecv_sem.at[phase, chunk],
+            device_id=device, device_id_type=MESH,
         )
 
-    def to_partner(c):
-        return pltpu.make_async_remote_copy(
-            partial.at[c], far_grad.at[c], gsend_sem.at[1, c], grecv_sem.at[1, c],
-            device_id={"shot": partner}, device_id_type=MESH,
-        )
+    def to_sibling():
+        return gradient_copy(0, 0, grad.at[pl.ds(other, 4)], near_grad.at[pl.ds(0, 4)], {"shot": sibling})
+
+    def to_partner():
+        return gradient_copy(1, 0, partial.at[pl.ds(0, 4)], far_grad.at[pl.ds(0, 4)], {"shot": partner})
 
     def to_passer():
-        return pltpu.make_async_remote_copy(
-            partial.at[0], passing, psend_sem.at[0], precv_sem.at[0],
-            device_id={"shot": partner, "dom": inside}, device_id_type=MESH,
-        )
+        return gradient_copy(3, 0, partial.at[pl.ds(0, 4)], passing, {"shot": partner, "dom": inside})
 
     def pass_on():
-        return pltpu.make_async_remote_copy(
-            passing, far_grad.at[0], psend_sem.at[1], precv_sem.at[1],
-            device_id={"dom": outside}, device_id_type=MESH,
-        )
-
-    def total_to_sibling(c):
-        return pltpu.make_async_remote_copy(
-            gradient.at[pl.ds(mine[c], 4)], gradient.at[pl.ds(mine[c], 4)], gsend_sem.at[2, c], grecv_sem.at[2, c],
-            device_id={"shot": sibling}, device_id_type=MESH,
-        )
-
-    def sum_near(c):
-        to_sibling(c).wait_recv()
+        return gradient_copy(4, 0, passing, far_grad.at[pl.ds(0, 4)], {"dom": outside})
+
+    def total_to_sibling():
+        place_of = gradient.at[pl.ds(mine, 4)]
+        return gradient_copy(2, 0, place_of, place_of, {"shot": sibling})
+
+    def edge_to_sibling(j):
+        return gradient_copy(0, 1 + j, grad.at[other_edge + j], near_grad.at[4 + j], {"shot": sibling})
+
+    def edge_to_partner(j):
+        return gradient_copy(1, 1 + j, partial.at[4 + j], far_grad.at[4 + j], {"shot": partner})
+
+    def edge_total_to_sibling(j):
+        place_of = gradient.at[mine_edge + j]
+        return gradient_copy(2, 1 + j, place_of, place_of, {"shot": sibling})
+
+    def sum_near():
+        to_sibling().wait_recv()
 
         def one(j, _):
-            partial[c, j] = grad[mine[c] + j] + near_grad[c, j]
+            partial[j] = grad[mine + j] + near_grad[j]
             return 0
 
         lax.fori_loop(0, 4, one, 0)
-        if c == 1:
-            to_partner(c).start()
-        else:
-            @pl.when(at_end)
-            def _():
-                to_passer().start()
-
-            @pl.when(jnp.logical_not(at_end))
-            def _():
-                to_partner(c).start()
-
-    def sum_far(c):
-        if c == 1:
-            to_partner(c).wait_recv()
-        else:
-            @pl.when(at_end)
-            def _():
-                pass_on().wait_recv()
-
-            @pl.when(jnp.logical_not(at_end))
-            def _():
-                to_partner(c).wait_recv()
+
+        @pl.when(at_end)
+        def _():
+            to_passer().start()
+
+        @pl.when(jnp.logical_not(at_end))
+        def _():
+            to_partner().start()
+
+    def sum_far():
+        @pl.when(at_end)
+        def _():
+            pass_on().wait_recv()
+
+        @pl.when(jnp.logical_not(at_end))
+        def _():
+            to_partner().wait_recv()
 
         def one(j, _):
-            gradient[mine[c] + j] = (partial[c, j] + far_grad[c, j]) * (1.0 / scale)
+            gradient[mine + j] = (partial[j] + far_grad[j]) * (1.0 / scale)
             return 0
 
         lax.fori_loop(0, 4, one, 0)
-        total_to_sibling(c).start()
+        total_to_sibling().start()
+
+    def sum_near_edge():
+        for j in range(4):
+            edge_to_sibling(j).wait_recv()
+            partial[4 + j] = grad[mine_edge + j] + near_grad[4 + j]
+            edge_to_partner(j).start()
+
+    def sum_far_edge():
+        for j in range(4):
+            edge_to_partner(j).wait_recv()
+            gradient[mine_edge + j] = (partial[4 + j] + far_grad[4 + j]) * (1.0 / scale)
+            edge_total_to_sibling(j).start()
 
     loads[2].wait()
     across_stage(ue.at[0], yzf)
@@ -396,6 +416,8 @@
         if n < 3:
             send_high(n + 1)
             across_stage(ue.at[n + 1], yzf)
+            if n == 2:
+                lax.fori_loop(4, planes - 4, combine, 0)
             middle(forward_group, n + 1)
         if n == 0:
             loads[4].wait()
@@ -403,20 +425,18 @@
             across_stage(se.at[0], yza)
             middle(adjoint_group, 0)
         if n == 2:
-            lax.fori_loop(4, planes - 4, combine, 0)
-            to_sibling(0).start()
-            sum_near(0)
+            to_sibling().start()
+            sum_near()
         if n == 3:
-            lax.fori_loop(0, 4, combine, 0)
-            lax.fori_loop(planes - 4, planes, combine, 0)
-            to_sibling(1).start()
+            for j in range(4):
+                edge_to_sibling(j).start()
 
             @pl.when(passes)
             def _():
                 to_passer().wait_recv()
                 pass_on().start()
 
-            sum_near(1)
+            sum_near_edge()
         if n == 1:
             lax.fori_loop(1, 2, inject_step, 0)
         wait_low(n + 4)
@@ -432,11 +452,15 @@
         if n < 3:
             across_stage(se.at[n + 1], yza)
             middle(adjoint_group, n + 1)
-    sum_far(0)
-    sum_far(1)
-
-    for c in range(2):
-        total_to_sibling(c).wait_recv()
+        if n == 2:
+            lax.fori_loop(0, 4, combine, 0)
+            lax.fori_loop(planes - 4, planes, combine, 0)
+    sum_far()
+    sum_far_edge()
+
+    total_to_sibling().wait_recv()
+    for j in range(4):
+        edge_total_to_sibling(j).wait_recv()
     for e in range(8):
         @pl.when(has_low)
         def _():
@@ -445,9 +469,8 @@
         @pl.when(has_high)
         def _():
             to_high(e, high_edge(e)).wait_send()
-    for c in range(2):
-        to_sibling(c).wait_send()
-        total_to_sibling(c).wait_send()
+    to_sibling().wait_send()
+    total_to_sibling().wait_send()
 
     @pl.when(at_end)
     def _():
@@ -459,9 +482,29 @@
 
     @pl.when(jnp.logical_not(at_end))
     def _():
-        to_partner(0).wait_send()
-
-    to_partner(1).wait_send()
+        to_partner().wait_send()
+
+    for j in range(4):
+        edge_to_sibling(j).wait_send()
+        edge_to_partner(j).wait_send()
+        edge_total_to_sibling(j).wait_send()
+
+
+def write(*refs):
+    sems = refs[6]
+    copies = []
+    for k in range(3):
+        source_ref, target_ref = refs[k], refs[k + 3]
+        if k < 2:
+            source_ref, target_ref = source_ref.at[0], target_ref.at[0]
+        size = source_ref.shape[0] // 4
+        for part in range(4):
+            piece = pl.ds(part * size, size)
+            copies.append(pltpu.make_async_copy(source_ref.at[piece], target_ref.at[piece], sems.at[k, part]))
+    for copy in copies:
+        copy.start()
+    for copy in copies:
+        copy.wait()
 
 
 def per_device(
@@ -474,23 +517,27 @@
     field = (planes, depth, across)
     extended = (4, planes + 8, depth, across)
     whole = pl.BlockSpec(memory_space=pltpu.HBM)
-    scalars = pl.BlockSpec(memory_space=pltpu.SMEM)
     vectors = pl.BlockSpec(memory_space=pltpu.VMEM)
-    return pl.pallas_call(
+    results = pl.pallas_call(
         functools.partial(kernel, doms),
         out_shape=(
             pltpu.VMEM(block, F32),
             pltpu.VMEM(block, F32),
             pltpu.VMEM(field, F32),
         ),
-        in_specs=[whole] * 5 + [scalars] * 3 + [vectors] * 2,
+        in_specs=[whole] * 10,
         out_specs=(vectors, vectors, vectors),
         scratch_shapes=[
+            pltpu.SMEM(table.shape, F32),
+            pltpu.SMEM(source_index.shape, jnp.int32),
+            pltpu.SMEM(wavelet.shape, F32),
+            pltpu.VMEM((3, 1, recs), jnp.int32),
+            pltpu.VMEM(residual.shape[1:], F32),
             pltpu.VMEM(extended, F32),
             pltpu.VMEM(field, F32),
             pltpu.VMEM(extended, F32),
             pltpu.VMEM((5,) + field, F32),
-            pltpu.VMEM((4,) + field, F32),
+            pltpu.VMEM((3,) + field, F32),
             pltpu.VMEM(field, F32),
             pltpu.VMEM(field, jnp.int32),
             pltpu.VMEM(field, F32),
@@ -503,17 +550,15 @@
             pltpu.VMEM((4,) + field, F32),
             pltpu.VMEM((depth, across), F32),
             pltpu.VMEM(field, F32),
-            pltpu.VMEM((2, 4, depth, across), F32),
-            pltpu.VMEM((2, 4, depth, across), F32),
-            pltpu.VMEM((2, 4, depth, across), F32),
+            pltpu.VMEM((8, depth, across), F32),
+            pltpu.VMEM((8, depth, across), F32),
+            pltpu.VMEM((8, depth, across), F32),
             pltpu.VMEM((4, depth, across), F32),
-            pltpu.SemaphoreType.DMA((5,)),
+            pltpu.SemaphoreType.DMA((10,)),
             pltpu.SemaphoreType.DMA((2, 8)),
             pltpu.SemaphoreType.DMA((2, 8)),
-            pltpu.SemaphoreType.DMA((3, 2)),
-            pltpu.SemaphoreType.DMA((3, 2)),
-            pltpu.SemaphoreType.DMA((2,)),
-            pltpu.SemaphoreType.DMA((2,)),
+            pltpu.SemaphoreType.DMA((5, 5)),
+            pltpu.SemaphoreType.DMA((5, 5)),
         ],
         compiler_params=pltpu.CompilerParams(
             collective_id=0, has_side_effects=True, vmem_limit_bytes=60 << 20
@@ -523,6 +568,16 @@
         wave_before, wave_current, adjoint_far, adjoint_near, labels, table,
         source_index, wavelet, jnp.transpose(receiver_index, (2, 0, 1)), residual[0],
     )
+    held = [pltpu.with_memory_space_constraint(result, pltpu.VMEM) for result in results]
+    return pl.pallas_call(
+        write,
+        out_shape=tuple(jax.ShapeDtypeStruct(result.shape, F32) for result in results),
+        in_specs=[vectors] * 3,
+        out_specs=(whole,) * 3,
+        scratch_shapes=[pltpu.SemaphoreType.DMA((3, 4))],
+        compiler_params=pltpu.CompilerParams(vmem_limit_bytes=1 << 20),
+        name="write",
+    )(*held)
 
 
 def solution(mesh):

time: 69.3 us -> 67.7 us (0.977)
  local copies, waits for them, and re-layouts: 2.91 us -> 0 us
  Pallas kernels: 65.6 us -> 66.9 us
    unnamed x3 -> x0, local copies, waits for them, and re-layouts: 2.91 us -> none
    pallas_call x0 -> x1, Pallas kernels: none -> 1.76 us  [per_device(): pl.pallas_call(write, out_shape=tuple((jax.ShapeDtypeStruct(result.shape,...]
where the time goes in v3:
time: 67.7 us; the launch traced here: 67.6 us
  Pallas kernels  66.9 us (99%)
    pallas_call x1, Pallas kernels, per_device(): pl.pallas_call(functools.partial(kernel, doms), out_shape=(pltpu.VMEM(blo...  65.2 us
    pallas_call x1, Pallas kernels, per_device(): pl.pallas_call(write, out_shape=tuple((jax.ShapeDtypeStruct(result.shape,...  1.76 us

profile of v3, /device:TPU:7, one launch (start us, length us, event | category | flops | bytes accessed | tf_op | source)
XLA Modules:
  0.0 67.6 jit_solution(11226863413487755192)
XLA Ops:
  0.6 65.2 %window.1 = (f32[1,16,64,256]{3,2,1,0:T(8,128)S(1)}, f32[1,16,64,256]{3,2,1,0:T(8,128)S(1)}, f32[16,64,256]{2,1,0:T(8,128)S(1)}) custom-call(f32[1,16,64,256]{3,2,1,0:T(8,128)} %before_hbm.1, f32[1,16,64,256]{3,2,1,0:T(8,128)} %current_hbm.1, f32[1,16,64,256]{3,2,1,0:T(8,128)} %far_hbm.1, f32[1,16,64,256]{3,2,1,0:T(8,128)} %near_hbm.1, ...), custom_call_target="tpu_custom_call" | custom-call | tf_op jit(solution)/shard_map/window/pallas_call | solution.py:521
  65.8 1.8 %write.1 = (f32[1,16,64,256]{3,2,1,0:T(8,128)}, f32[1,16,64,256]{3,2,1,0:T(8,128)}, f32[16,64,256]{2,1,0:T(8,128)}) custom-call(f32[1,16,64,256]{3,2,1,0:T(8,128)S(1)} %get-tuple-element.6.refs_0_, f32[1,16,64,256]{3,2,1,0:T(8,128)S(1)} %get-tuple-element.7.refs_1_, f32[16,64,256]{2,1,0:T(8,128)S(1)} %get-tuple-element.8.refs_2_), custom_call_target="tpu_custom_call" | custom-call | tf_op jit(solution)/shard_map/write/pallas_call | solution.py:572

commit v4 on v3

--- a/solution.py
+++ b/solution.py
@@ -27,15 +27,13 @@
     return high, middle, low
 
 
-def band(rows, columns, block):
-    row = lax.broadcasted_iota(jnp.int32, (rows, columns), 0)
-    column = lax.broadcasted_iota(jnp.int32, (rows, columns), 1)
+def band(size):
+    row = lax.broadcasted_iota(jnp.int32, (size, size), 0)
+    column = lax.broadcasted_iota(jnp.int32, (size, size), 1)
     away = jnp.abs(row - column)
-    result = jnp.zeros((rows, columns), F32)
+    result = jnp.zeros((size, size), F32)
     for k in range(1, 5):
         result = jnp.where(away == k, sides[k - 1], result)
-    if block:
-        result = jnp.where(row // block == column // block, result, 0.0)
     return result.astype(BF16)
 
 
@@ -44,7 +42,7 @@
     before_hbm, current_hbm, far_hbm, near_hbm, labels_hbm,
     table_hbm, source_hbm, wavelet_hbm, receivers_hbm, residual_hbm,
     final, first, gradient,
-    table, source, wavelet, receivers, residual, ue, u0, se, aa, lap, rate, labels, yzf, yza, stack, along_y, along_z,
+    table, source, wavelet, receivers, residual, ue, u0, se, aa, lap, rate, labels, yzf, yza, wide, tall, along_y, along_z,
     onehot, amounts, inject, spot, grad, near_grad, far_grad, partial, passing,
     load_sem, send_sem, recv_sem, gsend_sem, grecv_sem,
 ):
@@ -130,28 +128,31 @@
             return current_hbm.at[0, pl.ds(planes - 4, 4)]
         return (ue.at[e] if e < 4 else se.at[e - 4]).at[pl.ds(planes, 4)]
 
-    def send_low(e):
-        @pl.when(has_low)
+    def send(e, high):
+        @pl.when(jnp.logical_not(high) & has_low)
         def _():
             to_low(e, low_edge(e)).start()
 
-    def send_high(e):
-        @pl.when(has_high)
+        @pl.when(high & has_high)
         def _():
             to_high(e, high_edge(e)).start()
 
-    def wait_low(e):
-        @pl.when(has_low)
+    def wait(e, high):
+        @pl.when(jnp.logical_not(high) & has_low)
         def _():
             to_high(e, high_edge(e)).wait_recv()
 
-    def wait_high(e):
-        @pl.when(has_high)
+        @pl.when(high & has_high)
         def _():
             to_low(e, low_edge(e)).wait_recv()
 
-    send_low(0)
-    send_high(0)
+    order = (place == 0, place != 0)
+
+    def edge_group(high):
+        return jnp.where(high, groups - 1, 0)
+
+    for high in order:
+        send(0, high)
 
     @pl.when(dom == 0)
     def _():
@@ -186,16 +187,15 @@
     def first_group(base):
         lax.fori_loop(0, 4, lambda j, c: (first_plane(base + j), c)[1], 0)
 
-    first_group(0)
-    send_low(4)
-    first_group(planes - 4)
-    send_high(4)
+    for high in order:
+        first_group(4 * edge_group(high))
+        send(4, high)
     lax.fori_loop(4, planes - 4, lambda p, c: (first_plane(p), c)[1], 0)
 
-    along_y[...] = band(across, across, 0)
-    plane_band = band(4 * depth, 4 * depth, depth)
+    row_band, column_band = band(across), band(depth)
     for k in range(3):
-        along_z[:, k * 4 * depth:(k + 1) * 4 * depth] = plane_band
+        along_y[k * across:(k + 1) * across, :] = row_band
+        along_z[:, k * depth:(k + 1) * depth] = column_band
 
     for k in range(6, 10):
         loads[k].wait()
@@ -205,24 +205,23 @@
     source_plane = source[0, 0] - dom * planes
 
     def across_stage(ext, out):
-        def group(g, _):
-            for q in range(4):
-                def rows(i, _, q=q):
-                    at = pl.multiple_of(i * 16, 16)
-                    parts = split(ext[4 + 4 * g + q, pl.ds(at, 16), :])
-                    for k in range(3):
-                        stack[pl.ds(pl.multiple_of(at + (4 * k + q) * depth, 16), 16), :] = parts[k]
-                    return 0
-
-                lax.fori_loop(0, depth // 16, rows, 0, unroll=True)
-            size = 4 * depth
-            in_y = jnp.dot(stack[...], along_y[...], preferred_element_type=F32)
-            in_z = jnp.dot(along_z[...], stack[...], preferred_element_type=F32)
-            both = (in_y[2 * size:] + in_y[size:2 * size]) + in_y[:size] + in_z
-            out[pl.ds(4 * g, 4)] = both.reshape(4, depth, across)
-            return 0
-
-        lax.fori_loop(0, groups, group, 0)
+        def pair(i, _):
+            for h in range(2):
+                g = 2 * i + h
+                for q in range(4):
+                    for part in range(depth // 16):
+                        at = 16 * part
+                        terms = split(ext[4 + 4 * g + q, at:at + 16, :])
+                        for k in range(3):
+                            wide[h, q * depth + at:q * depth + at + 16, k * across:(k + 1) * across] = terms[k]
+                            tall[h, q, k * depth + at:k * depth + at + 16, :] = terms[k]
+                in_y = jnp.dot(wide[h], along_y[...], preferred_element_type=F32)
+                for q in range(4):
+                    in_z = jnp.dot(along_z[...], tall[h, q], preferred_element_type=F32)
+                    out[4 * g + q] = in_y[q * depth:(q + 1) * depth] + in_z
+            return 0
+
+        lax.fori_loop(0, groups // 2, pair, 0)
 
     def laplace(planes_of, j, rest):
         result = rest + centre * planes_of[j + 4]
@@ -284,30 +283,30 @@
 
     lax.fori_loop(0, planes * depth // 16, onehot_rows, 0)
 
-    def inject_step(n, _):
-        value = residual[pl.ds(n, 1), :]
-        parts = [part.astype(F32) for part in split(value)]
+    def inject_step(n):
+        value = residual[n:n + 1, :]
+        high = value.astype(BF16).astype(F32)
+        parts = (high, (value - high).astype(BF16).astype(F32))
 
         def columns(i, _):
             at = pl.multiple_of(i * 16, 16)
             here = lax.broadcasted_iota(jnp.int32, (16, recs), 0) + at == receivers[2]
-            for k in range(3):
+            for k in range(2):
                 amounts[pl.ds(pl.multiple_of(at + k * across, 16), 16), :] = jnp.where(here, parts[k], 0.0).astype(BF16)
             return 0
 
         lax.fori_loop(0, across // 16, columns, 0)
 
-        def group(g, _):
-            rows = pl.ds(pl.multiple_of(g * 4 * depth, 4 * depth), 4 * depth)
+        def half(i, _):
+            rows = pl.ds(pl.multiple_of(i * 8 * depth, 8 * depth), 8 * depth)
             spread = lax.dot_general(
                 onehot[rows, :], amounts[...], (((1,), (1,)), ((), ())), preferred_element_type=F32
             )
-            both = (spread[:, 2 * across:] + spread[:, across:2 * across]) + spread[:, :across]
-            inject[n, pl.ds(4 * g, 4)] = both.reshape(4, depth, across)
-            return 0
-
-        lax.fori_loop(0, groups, group, 0)
-        return 0
+            both = spread[:, across:] + spread[:, :across]
+            inject[n, pl.ds(8 * i, 8)] = both.reshape(8, depth, across)
+            return 0
+
+        lax.fori_loop(0, planes // 8, half, 0)
 
     def combine(p, _):
         def rows(i, _):
@@ -389,11 +388,20 @@
         lax.fori_loop(0, 4, one, 0)
         total_to_sibling().start()
 
-    def sum_near_edge():
-        for j in range(4):
-            edge_to_sibling(j).wait_recv()
-            partial[4 + j] = grad[mine_edge + j] + near_grad[4 + j]
-            edge_to_partner(j).start()
+    def sum_near_edge(high):
+        owner = high == (core == 1)
+
+        @pl.when(jnp.logical_not(owner))
+        def _():
+            for j in range(4):
+                edge_to_sibling(j).start()
+
+        @pl.when(owner)
+        def _():
+            for j in range(4):
+                edge_to_sibling(j).wait_recv()
+                partial[4 + j] = grad[mine_edge + j] + near_grad[4 + j]
+                edge_to_partner(j).start()
 
     def sum_far_edge():
         for j in range(4):
@@ -405,58 +413,49 @@
     across_stage(ue.at[0], yzf)
     loads[3].wait()
     middle(forward_group, 0)
+    inject_step(3)
+    loads[4].wait()
+    across_stage(se.at[0], yza)
+    middle(adjoint_group, 0)
 
     for n in range(4):
-        wait_low(n)
-        forward_group(n, 0)
+        for high in order:
+            wait(n, high)
+            forward_group(n, edge_group(high))
+            if n < 3:
+                send(n + 1, high)
+            else:
+                sum_near_edge(high)
         if n < 3:
-            send_low(n + 1)
-        wait_high(n)
-        forward_group(n, groups - 1)
-        if n < 3:
-            send_high(n + 1)
             across_stage(ue.at[n + 1], yzf)
             if n == 2:
                 lax.fori_loop(4, planes - 4, combine, 0)
             middle(forward_group, n + 1)
-        if n == 0:
-            loads[4].wait()
-            lax.fori_loop(3, 4, inject_step, 0)
-            across_stage(se.at[0], yza)
-            middle(adjoint_group, 0)
         if n == 2:
             to_sibling().start()
             sum_near()
         if n == 3:
-            for j in range(4):
-                edge_to_sibling(j).start()
-
             @pl.when(passes)
             def _():
                 to_passer().wait_recv()
                 pass_on().start()
-
-            sum_near_edge()
+        if n < 2:
+            inject_step(2 - n)
+        for high in order:
+            wait(n + 4, high)
+            adjoint_group(n, edge_group(high))
+            if n < 3:
+                send(n + 5, high)
         if n == 1:
-            lax.fori_loop(1, 2, inject_step, 0)
-        wait_low(n + 4)
-        adjoint_group(n, 0)
-        if n < 3:
-            send_low(n + 5)
-        wait_high(n + 4)
-        adjoint_group(n, groups - 1)
-        if n < 3:
-            send_high(n + 5)
-        if n < 2:
-            lax.fori_loop(2 - 2 * n, 3 - 2 * n, inject_step, 0)
+            inject_step(0)
         if n < 3:
             across_stage(se.at[n + 1], yza)
             middle(adjoint_group, n + 1)
         if n == 2:
             lax.fori_loop(0, 4, combine, 0)
             lax.fori_loop(planes - 4, planes, combine, 0)
+    sum_far_edge()
     sum_far()
-    sum_far_edge()
 
     total_to_sibling().wait_recv()
     for j in range(4):
@@ -542,11 +541,12 @@
             pltpu.VMEM(field, jnp.int32),
             pltpu.VMEM(field, F32),
             pltpu.VMEM(field, F32),
-            pltpu.VMEM((12 * depth, across), BF16),
-            pltpu.VMEM((across, across), BF16),
-            pltpu.VMEM((4 * depth, 12 * depth), BF16),
+            pltpu.VMEM((2, 4 * depth, 3 * across), BF16),
+            pltpu.VMEM((2, 4, 3 * depth, across), BF16),
+            pltpu.VMEM((3 * across, across), BF16),
+            pltpu.VMEM((depth, 3 * depth), BF16),
             pltpu.VMEM((planes * depth, recs), BF16),
-            pltpu.VMEM((3 * across, recs), BF16),
+            pltpu.VMEM((2 * across, recs), BF16),
             pltpu.VMEM((4,) + field, F32),
             pltpu.VMEM((depth, across), F32),
             pltpu.VMEM(field, F32),

time: 67.7 us -> 67.3 us (level)
  no operation moved by 1% of the time
where the time goes in v4:
time: 67.3 us; the launch traced here: 67.2 us
  Pallas kernels  66.6 us (99%)
    pallas_call x1, Pallas kernels, per_device(): pl.pallas_call(functools.partial(kernel, doms), out_shape=(pltpu.VMEM(blo...  64.8 us
    pallas_call x1, Pallas kernels, per_device(): pl.pallas_call(write, out_shape=tuple((jax.ShapeDtypeStruct(result.shape,...  1.76 us

profile of v4, /device:TPU:7, one launch (start us, length us, event | category | flops | bytes accessed | tf_op | source)
XLA Modules:
  0.0 67.2 jit_solution(17434986971438596004)
XLA Ops:
  0.6 64.8 %window.1 = (f32[1,16,64,256]{3,2,1,0:T(8,128)S(1)}, f32[1,16,64,256]{3,2,1,0:T(8,128)S(1)}, f32[16,64,256]{2,1,0:T(8,128)S(1)}) custom-call(f32[1,16,64,256]{3,2,1,0:T(8,128)} %before_hbm.1, f32[1,16,64,256]{3,2,1,0:T(8,128)} %current_hbm.1, f32[1,16,64,256]{3,2,1,0:T(8,128)} %far_hbm.1, f32[1,16,64,256]{3,2,1,0:T(8,128)} %near_hbm.1, ...), custom_call_target="tpu_custom_call" | custom-call | tf_op jit(solution)/shard_map/window/pallas_call | solution.py:520
  65.4 1.8 %write.1 = (f32[1,16,64,256]{3,2,1,0:T(8,128)}, f32[1,16,64,256]{3,2,1,0:T(8,128)}, f32[16,64,256]{2,1,0:T(8,128)}) custom-call(f32[1,16,64,256]{3,2,1,0:T(8,128)S(1)} %get-tuple-element.6.refs_0_, f32[1,16,64,256]{3,2,1,0:T(8,128)S(1)} %get-tuple-element.7.refs_1_, f32[16,64,256]{2,1,0:T(8,128)S(1)} %get-tuple-element.8.refs_2_), custom_call_target="tpu_custom_call" | custom-call | tf_op jit(solution)/shard_map/write/pallas_call | solution.py:572

commit v5 on v4

--- a/solution.py
+++ b/solution.py
@@ -336,10 +336,14 @@
         return gradient_copy(1, 0, partial.at[pl.ds(0, 4)], far_grad.at[pl.ds(0, 4)], {"shot": partner})
 
     def to_passer():
-        return gradient_copy(3, 0, partial.at[pl.ds(0, 4)], passing, {"shot": partner, "dom": inside})
+        return gradient_copy(3, 0, partial.at[pl.ds(0, 3)], passing, {"shot": partner, "dom": inside})
+
+    def rest_to_partner():
+        rest = pl.ds(3, 1)
+        return gradient_copy(3, 1, partial.at[rest], far_grad.at[rest], {"shot": partner})
 
     def pass_on():
-        return gradient_copy(4, 0, passing, far_grad.at[pl.ds(0, 4)], {"dom": outside})
+        return gradient_copy(4, 0, passing, far_grad.at[pl.ds(0, 3)], {"dom": outside})
 
     def total_to_sibling():
         place_of = gradient.at[pl.ds(mine, 4)]
@@ -367,6 +371,7 @@
         @pl.when(at_end)
         def _():
             to_passer().start()
+            rest_to_partner().start()
 
         @pl.when(jnp.logical_not(at_end))
         def _():
@@ -375,6 +380,7 @@
     def sum_far():
         @pl.when(at_end)
         def _():
+            rest_to_partner().wait_recv()
             pass_on().wait_recv()
 
         @pl.when(jnp.logical_not(at_end))
@@ -474,6 +480,7 @@
     @pl.when(at_end)
     def _():
         to_passer().wait_send()
+        rest_to_partner().wait_send()
 
     @pl.when(passes)
     def _():
@@ -553,7 +560,7 @@
             pltpu.VMEM((8, depth, across), F32),
             pltpu.VMEM((8, depth, across), F32),
             pltpu.VMEM((8, depth, across), F32),
-            pltpu.VMEM((4, depth, across), F32),
+            pltpu.VMEM((3, depth, across), F32),
             pltpu.SemaphoreType.DMA((10,)),
             pltpu.SemaphoreType.DMA((2, 8)),
             pltpu.SemaphoreType.DMA((2, 8)),

time: 67.3 us -> 66.6 us (0.990); the launches traced: 67.2 us -> 65.7 us
  Pallas kernels: 66.6 us -> 65 us
    pallas_call x1, Pallas kernels: 64.8 us -> 63.3 us  [per_device(): pl.pallas_call(functools.partial(kernel, doms), out_shape=(pltpu.VMEM(blo...]
where the time goes in v5:
time: 66.6 us; the launch traced here: 65.7 us
  Pallas kernels  65 us (98%)
    pallas_call x1, Pallas kernels, per_device(): pl.pallas_call(functools.partial(kernel, doms), out_shape=(pltpu.VMEM(blo...  63.3 us
    pallas_call x1, Pallas kernels, per_device(): pl.pallas_call(write, out_shape=tuple((jax.ShapeDtypeStruct(result.shape,...  1.76 us

profile of v5, /device:TPU:7, one launch (start us, length us, event | category | flops | bytes accessed | tf_op | source)
XLA Modules:
  0.0 65.7 jit_solution(10035861561752673682)
XLA Ops:
  0.6 63.3 %window.1 = (f32[1,16,64,256]{3,2,1,0:T(8,128)S(1)}, f32[1,16,64,256]{3,2,1,0:T(8,128)S(1)}, f32[16,64,256]{2,1,0:T(8,128)S(1)}) custom-call(f32[1,16,64,256]{3,2,1,0:T(8,128)} %before_hbm.1, f32[1,16,64,256]{3,2,1,0:T(8,128)} %current_hbm.1, f32[1,16,64,256]{3,2,1,0:T(8,128)} %far_hbm.1, f32[1,16,64,256]{3,2,1,0:T(8,128)} %near_hbm.1, ...), custom_call_target="tpu_custom_call" | custom-call | tf_op jit(solution)/shard_map/window/pallas_call | solution.py:527
  63.9 1.8 %write.1 = (f32[1,16,64,256]{3,2,1,0:T(8,128)}, f32[1,16,64,256]{3,2,1,0:T(8,128)}, f32[16,64,256]{2,1,0:T(8,128)}) custom-call(f32[1,16,64,256]{3,2,1,0:T(8,128)S(1)} %get-tuple-element.6.refs_0_, f32[1,16,64,256]{3,2,1,0:T(8,128)S(1)} %get-tuple-element.7.refs_1_, f32[16,64,256]{2,1,0:T(8,128)S(1)} %get-tuple-element.8.refs_2_), custom_call_target="tpu_custom_call" | custom-call | tf_op jit(solution)/shard_map/write/pallas_call | solution.py:579

commit v6 on v5

--- a/solution.py
+++ b/solution.py
@@ -371,7 +371,6 @@
         @pl.when(at_end)
         def _():
             to_passer().start()
-            rest_to_partner().start()
 
         @pl.when(jnp.logical_not(at_end))
         def _():
@@ -441,6 +440,10 @@
             to_sibling().start()
             sum_near()
         if n == 3:
+            @pl.when(at_end)
+            def _():
+                rest_to_partner().start()
+
             @pl.when(passes)
             def _():
                 to_passer().wait_recv()

time: 66.6 us -> 66.6 us (level)
  no operation moved by 1% of the time
where the time goes in v6:
time: 66.6 us; the launch traced here: 65.7 us
  Pallas kernels  65 us (98%)
    pallas_call x1, Pallas kernels, per_device(): pl.pallas_call(functools.partial(kernel, doms), out_shape=(pltpu.VMEM(blo...  63.3 us
    pallas_call x1, Pallas kernels, per_device(): pl.pallas_call(write, out_shape=tuple((jax.ShapeDtypeStruct(result.shape,...  1.76 us

profile of v6, /device:TPU:7, one launch (start us, length us, event | category | flops | bytes accessed | tf_op | source)
XLA Modules:
  0.0 65.7 jit_solution(208021405138182888)
XLA Ops:
  0.6 63.3 %window.1 = (f32[1,16,64,256]{3,2,1,0:T(8,128)S(1)}, f32[1,16,64,256]{3,2,1,0:T(8,128)S(1)}, f32[16,64,256]{2,1,0:T(8,128)S(1)}) custom-call(f32[1,16,64,256]{3,2,1,0:T(8,128)} %before_hbm.1, f32[1,16,64,256]{3,2,1,0:T(8,128)} %current_hbm.1, f32[1,16,64,256]{3,2,1,0:T(8,128)} %far_hbm.1, f32[1,16,64,256]{3,2,1,0:T(8,128)} %near_hbm.1, ...), custom_call_target="tpu_custom_call" | custom-call | tf_op jit(solution)/shard_map/window/pallas_call | solution.py:530
  63.9 1.8 %write.1 = (f32[1,16,64,256]{3,2,1,0:T(8,128)}, f32[1,16,64,256]{3,2,1,0:T(8,128)}, f32[16,64,256]{2,1,0:T(8,128)}) custom-call(f32[1,16,64,256]{3,2,1,0:T(8,128)S(1)} %get-tuple-element.6.refs_0_, f32[1,16,64,256]{3,2,1,0:T(8,128)S(1)} %get-tuple-element.7.refs_1_, f32[16,64,256]{2,1,0:T(8,128)S(1)} %get-tuple-element.8.refs_2_), custom_call_target="tpu_custom_call" | custom-call | tf_op jit(solution)/shard_map/write/pallas_call | solution.py:582
